TPU v7x, 32 devices: a whole 2x2x4 slice. The times are simulated.
32 devices in a mesh: gx: 8 (over z, core), gy: 4 (over y, x).
Axes of the slice: x: 2, y: 2, z: 4, core: 2. Of those that a mesh axis runs over, the one named last changes fastest.
Arguments:
- dtn_maps: float32 [8, 4, 1024, 1024], P('gx', 'gy'), may hold values from -8 to 25, as said below
- flux_part: float32 [8, 4, 1024, 32], P('gx', 'gy'), may hold values from -6 to 6
- outer_values: float32 [8, 4, 512, 32], P('gx', 'gy'), may hold values from -6 to 6
Outputs:
- merged_map: float32 [8, 4, 512, 2048], P('gx', 'gy')
- merged_flux: float32 [8, 4, 512, 32], P('gx', 'gy')
- box_values: float32 [8, 4, 1024, 32], P('gx', 'gy')
Inputs may be any that keep to these rules, and one draw needn't show every extreme that they name: `dtn_maps`: each box's map is symmetric positive definite.
All inputs are finite; a program needn't handle non-finite values.
Results may differ from a plain program's by a relative error of at most 0.00005.
Values sent between devices are 32-bit elements; how exact they have to be, the bound alone decides.
A program may use at most 128 MiB of HBM per device.

v0:
```python
import jax
import jax.numpy as jnp
from jax import lax
from jax.sharding import PartitionSpec as P


def partner(value, axis, distance):
    mask = 2**distance
    pairs = [(source, source ^ mask) for source in range(lax.axis_size(axis))]
    return lax.ppermute(value, axis, pairs)


def product(left, right):
    return jnp.dot(left, right, precision=lax.Precision.HIGHEST, preferred_element_type=jnp.float32)


def invert_spd(matrix):
    factor = jnp.linalg.cholesky(matrix)
    identity = jnp.eye(matrix.shape[0], dtype=jnp.float32)
    halfway = lax.linalg.triangular_solve(factor, identity, left_side=True, lower=True)
    return lax.linalg.triangular_solve(
        factor, halfway, left_side=True, lower=True, transpose_a=True
    )


def arrange(mine_part, their_part, bit_value):
    return jnp.where(
        bit_value == 0, jnp.stack([mine_part, their_part]), jnp.stack([their_part, mine_part])
    )


def pick_cols(row_block, col_list):
    return row_block[:, jnp.array(col_list, dtype=jnp.int32)].reshape(row_block.shape[0], -1)


def on_device(dtn_maps, flux_part, outer_values):
    edge_len = dtn_maps.shape[2] // 4
    kept_len = 3 * edge_len
    zero_index = jnp.zeros((), jnp.int32)
    half_x = lax.axis_size("gx") // 2
    half_y = lax.axis_size("gy") // 2
    top_x = lax.axis_size("gx").bit_length() - 2
    top_y = lax.axis_size("gy").bit_length() - 2
    parity_x = lax.axis_index("gx") // half_x
    parity_y = lax.axis_index("gy") // half_y
    side_order = jnp.where(
        parity_x == 0,
        jnp.array([0, 2, 3, 1], dtype=jnp.int32),
        jnp.array([0, 1, 2, 3], dtype=jnp.int32),
    )
    inverse_order = jnp.where(
        parity_x == 0,
        jnp.array([0, 3, 1, 2], dtype=jnp.int32),
        jnp.array([0, 1, 2, 3], dtype=jnp.int32),
    )
    shaped = dtn_maps[0, 0].reshape(4, edge_len, 4, edge_len)
    ordered = jnp.take(jnp.take(shaped, side_order, axis=0), side_order, axis=2).reshape(
        4 * edge_len, 4 * edge_len
    )
    fluxes = jnp.take(flux_part[0, 0].reshape(4, edge_len, -1), side_order, axis=0).reshape(
        4 * edge_len, -1
    )
    own_ik = ordered[kept_len:, :kept_len]
    own_ii = ordered[kept_len:, kept_len:]
    own_hi = fluxes[kept_len:]
    other_ik, other_ii, other_hi = partner((own_ik, own_ii, own_hi), "gx", top_x)
    inverse = invert_spd(own_ii + other_ii)
    coupling = jnp.zeros((edge_len, 6 * edge_len), jnp.float32)
    coupling = lax.dynamic_update_slice(coupling, own_ik, (zero_index, kept_len * parity_x))
    coupling = lax.dynamic_update_slice(coupling, other_ik, (zero_index, kept_len * (1 - parity_x)))
    solved = product(inverse, coupling)
    solved_flux = product(inverse, own_hi + other_hi)
    own_ki = ordered[:kept_len, kept_len:]
    own_rows = lax.dynamic_update_slice(
        jnp.zeros((kept_len, 6 * edge_len), jnp.float32),
        ordered[:kept_len, :kept_len],
        (zero_index, kept_len * parity_x),
    ) - product(own_ki, solved)
    row_flux = fluxes[:kept_len] - product(own_ki, solved_flux)
    keep_table = jnp.array([[[0, 2], [1, 2]], [[0, 1], [1, 2]]], dtype=jnp.int32)
    inner_table = jnp.array([[1, 0], [2, 0]], dtype=jnp.int32)
    keep_rows = keep_table[parity_x, parity_y]
    inner_row = inner_table[parity_x, parity_y]
    stacked = own_rows.reshape(3, edge_len, 6 * edge_len)
    flux_stack = row_flux.reshape(3, edge_len, -1)
    send_rows = lax.dynamic_index_in_dim(stacked, inner_row, 0, keepdims=False)
    send_flux = lax.dynamic_index_in_dim(flux_stack, inner_row, 0, keepdims=False)
    near_rows, near_flux = partner((send_rows, send_flux), "gx", top_x)
    pair_rows = arrange(send_rows, near_rows, parity_x)
    pair_flux = arrange(send_flux, near_flux, parity_x)
    got_rows, got_flux = partner((pair_rows, pair_flux), "gy", top_y)
    all_rows = jnp.swapaxes(arrange(pair_rows, got_rows, parity_y), 0, 1)
    all_flux = jnp.swapaxes(arrange(pair_flux, got_flux, parity_y), 0, 1)
    lower_box = jnp.concatenate([all_rows[0, 0], all_rows[1, 0]], axis=0).reshape(
        2 * edge_len, 6, edge_len
    )
    upper_box = jnp.concatenate([all_rows[0, 1], all_rows[1, 1]], axis=0).reshape(
        2 * edge_len, 6, edge_len
    )
    block_inner = pick_cols(lower_box, [1, 5]) + pick_cols(upper_box, [0, 3])
    block_coupling = jnp.concatenate(
        [pick_cols(lower_box, [0, 2, 3, 4]), pick_cols(upper_box, [1, 2, 4, 5])], axis=1
    )
    block_inverse = invert_spd(block_inner)
    block_solve = product(block_inverse, block_coupling)
    block_fsum = jnp.concatenate(
        [all_flux[0, 0] + all_flux[0, 1], all_flux[1, 0] + all_flux[1, 1]], axis=0
    )
    block_fsolve = product(block_inverse, block_fsum)
    row_part = jnp.take(stacked, keep_rows, axis=0).reshape(2 * edge_len, 6, edge_len)
    box_cols = jnp.where(
        parity_y == 0,
        jnp.array([0, 2, 3, 4], dtype=jnp.int32),
        jnp.array([1, 2, 4, 5], dtype=jnp.int32),
    )
    inner_cols = jnp.where(
        parity_y == 0, jnp.array([1, 5], dtype=jnp.int32), jnp.array([0, 3], dtype=jnp.int32)
    )
    own_cols = jnp.take(row_part, box_cols, axis=1).reshape(2 * edge_len, 4 * edge_len)
    across = jnp.take(row_part, inner_cols, axis=1).reshape(2 * edge_len, 2 * edge_len)
    merged_map = lax.dynamic_update_slice(
        jnp.zeros((2 * edge_len, 8 * edge_len), jnp.float32),
        own_cols,
        (zero_index, 4 * edge_len * parity_y),
    ) - product(across, block_solve)
    merged_flux = jnp.take(flux_stack, keep_rows, axis=0).reshape(2 * edge_len, -1) - product(
        across, block_fsolve
    )
    outer = outer_values[0, 0]
    group_slot = parity_x + 2 * parity_y
    own_term = product(
        lax.dynamic_slice_in_dim(block_solve, 2 * edge_len * group_slot, 2 * edge_len, 1), outer
    )
    group_sum = own_term + partner(own_term, "gx", top_x)
    group_sum = group_sum + partner(group_sum, "gy", top_y)
    inner_values = -(group_sum + block_fsolve)
    own_inner = lax.dynamic_slice_in_dim(inner_values, edge_len * parity_x, edge_len, 0)
    boundary = jnp.zeros((3, edge_len, outer.shape[1]), jnp.float32)
    boundary = boundary.at[keep_rows].set(outer.reshape(2, edge_len, -1))
    boundary = boundary.at[inner_row].set(own_inner)
    boundary = boundary.reshape(kept_len, -1)
    pair_term = product(
        lax.dynamic_slice_in_dim(solved, kept_len * parity_x, kept_len, 1), boundary
    )
    pair_sum = pair_term + partner(pair_term, "gx", top_x)
    pair_inner = -(pair_sum + solved_flux)
    values = jnp.concatenate([boundary, pair_inner], axis=0).reshape(4, edge_len, -1)
    box_values = jnp.take(values, inverse_order, axis=0).reshape(4 * edge_len, -1)
    return (merged_map[None, None], merged_flux[None, None], box_values[None, None])


def solution(mesh):
    placed = (P("gx", "gy", None, None), P("gx", "gy", None, None), P("gx", "gy", None, None))
    return jax.shard_map(
        on_device,
        mesh=mesh,
        in_specs=placed,
        out_specs=(P("gx", "gy", None, None), P("gx", "gy", None, None), P("gx", "gy", None, None)),
        check_vma=False,
    )
```

profile of v0, /device:TPU:0, one launch (start us, length us, event | category | flops | bytes accessed | tf_op | source)
XLA Modules:
  0.0 571.6 jit_solution(4083366120679564716)
XLA Ops:
  1.3 5.6 reshape_squeeze.9
  11.8 5.0 gather_fusion
  21.5 4.9 gather_fusion.1
  26.4 5.2 copy.94
  31.7 5.1 copy.143
  70.0 6.1 %collective-permute-done = f32[256,256]{0,1:T(8,128)S(1)} collective-permute-done((f32[256,256]{0,1:T(8,128)}, f32[256,256]{0,1:T(8,128)S(1)}, u32[]{:S(2)}, u32[]{:S(2)}) %collective-permute-start) | collective-permute-done | bytes 262176 | tf_op jit(solution)/shard_map/ppermute | solution.py:10
  77.3 11.7 %cholesky.134 = f32[128,128]{1,0:T(8,128)S(1)} custom-call(f32[128,128]{1,0:T(8,128)S(1)} %cholesky.336), custom_call_target="Cholesky" | custom-call | tf_op jit(solution)/shard_map/jit(cholesky)/cholesky | solution.py:18
  89.1 9.8 %custom-call.46 = f32[1,128,128]{1,2,0:T(8,128)S(1)} custom-call(f32[1,128,128]{2,1,0:T(8,128)S(1)} %get-tuple-element.83), custom_call_target="InvertDiagBlocksLowerTriangular" | custom-call | tf_op jit(solution)/shard_map/jit(cholesky)/cholesky/custom-call.1 | solution.py:18
  99.3 11.7 %cholesky.144 = f32[128,128]{1,0:T(8,128)S(1)} custom-call(f32[128,128]{1,0:T(8,128)S(1)} %slice_subtract_fusion), custom_call_target="Cholesky" | custom-call | tf_op jit(solution)/shard_map/jit(cholesky)/cholesky | solution.py:18
  117.0 20.3 %custom-call.41 = f32[2,128,128]{1,2,0:T(8,128)S(1)} custom-call(f32[2,128,128]{2,1,0:T(8,128)S(1)} %get-tuple-element.24), custom_call_target="InvertDiagBlocksLowerTriangular" | custom-call | tf_op jit(solution)/shard_map/triangular_solve | solution.py:21
  144.0 7.0 %convolution_subtract_fusion = f32[768,1536]{1,0:T(8,128)S(1)} fusion(f32[768,1536]{1,0:T(8,128)} %constant_dynamic-update-slice_fusion.4, f32[256,1536]{1,0:T(8,128)S(1)} %fusion.43, f32[1024,1024]{0,1:T(8,128)} %copy-done.1), kind=kOutput, calls=%fused_computation.24 | convolution fusion | flops 3625058304 | bytes 11796480 | tf_op jit(solution)/shard_map/dot_general | solution.py:14
  155.1 65.5 %collective-permute-done.2 = f32[256,1536]{1,0:T(8,128)S(1)} collective-permute-done((f32[256,1536]{1,0:T(8,128)S(1)}, f32[256,1536]{1,0:T(8,128)S(1)}, u32[]{:S(2)}, u32[]{:S(2)}) %collective-permute-start.2) | collective-permute-done | bytes 1572896 | tf_op jit(solution)/shard_map/ppermute | solution.py:10
  235.0 58.3 %collective-permute-done.6 = f32[2,256,32]{1,0,2:T(2,128)S(1)} collective-permute-done((f32[2,256,32]{1,0,2:T(2,128)S(1)}, f32[2,256,32]{1,0,2:T(2,128)S(1)}, u32[]{:S(2)}, u32[]{:S(2)}) %collective-permute-start.6) | collective-permute-done | bytes 65568 | tf_op jit(solution)/shard_map/ppermute | solution.py:10
  364.5 11.7 %cholesky.274 = f32[128,128]{1,0:T(8,128)S(1)} custom-call(f32[128,128]{1,0:T(8,128)S(1)} %cholesky.339), custom_call_target="Cholesky" | custom-call | tf_op jit(solution)/shard_map/jit(cholesky)/cholesky | solution.py:18
  377.4 9.8 %custom-call.42 = f32[1,128,128]{1,2,0:T(8,128)S(1)} custom-call(f32[1,128,128]{2,1,0:T(8,128)S(1)} %get-tuple-element.79), custom_call_target="InvertDiagBlocksLowerTriangular" | custom-call | tf_op jit(solution)/shard_map/jit(cholesky)/cholesky | solution.py:18
  391.1 11.9 %cholesky.292 = f32[128,128]{1,0:T(8,128)S(1)} custom-call(f32[128,128]{1,0:T(8,128)S(1)} %cholesky.343), custom_call_target="Cholesky" | custom-call | tf_op jit(solution)/shard_map/jit(cholesky)/cholesky | solution.py:18
  404.9 9.8 %custom-call.43 = f32[1,128,128]{1,2,0:T(8,128)S(1)} custom-call(f32[1,128,128]{2,1,0:T(8,128)S(1)} %get-tuple-element.76), custom_call_target="InvertDiagBlocksLowerTriangular" | custom-call | tf_op jit(solution)/shard_map/jit(cholesky)/cholesky | solution.py:18
  418.0 11.7 %cholesky.313 = f32[128,128]{1,0:T(8,128)S(1)} custom-call(f32[128,128]{1,0:T(8,128)S(1)} %cholesky.348), custom_call_target="Cholesky" | custom-call | tf_op jit(solution)/shard_map/jit(cholesky)/cholesky | solution.py:18
  431.1 10.2 %custom-call.47 = f32[1,128,128]{1,2,0:T(8,128)S(1)} custom-call(f32[1,128,128]{2,1,0:T(8,128)S(1)} %get-tuple-element.73), custom_call_target="InvertDiagBlocksLowerTriangular" | custom-call | tf_op jit(solution)/shard_map/jit(cholesky)/cholesky/custom-call.1 | solution.py:18
  443.5 11.7 %cholesky.326 = f32[128,128]{1,0:T(8,128)S(1)} custom-call(f32[128,128]{1,0:T(8,128)S(1)} %convolution_subtract_fusion.13), custom_call_target="Cholesky" | custom-call | tf_op jit(solution)/shard_map/jit(cholesky)/cholesky | solution.py:18
  462.2 13.8 %while.4 = (s32[]{:T(128)}, f32[512,512]{1,0:T(8,128)}, s32[4,2]{0,1:T(2,128)S(1)}, f32[4,128,128]{2,1,0:T(8,128)}, s32[]{:T(128)}) while((s32[]{:T(128)}, f32[512,512]{1,0:T(8,128)}, s32[4,2]{0,1:T(2,128)S(1)}, f32[4,128,128]{2,1,0:T(8,128)}, s32[]{:T(128)}) %tuple.72), condition=%wide.while_cond.2, body=%wide.while_body.2.sunk | while | flops 2 | bytes 132705 | solution.py:21
  476.0 40.1 %custom-call.44 = f32[4,128,128]{1,2,0:T(8,128)S(1)} custom-call(f32[4,128,128]{2,1,0:T(8,128)} %get-tuple-element.32), custom_call_target="InvertDiagBlocksLowerTriangular" | custom-call | tf_op jit(solution)/shard_map/triangular_solve | solution.py:21
  539.0 8.5 %fusion.1 = f32[512,2048]{1,0:T(8,128)S(1)} fusion(f32[512,1024]{0,1:T(8,128)} %bitcast.224, f32[512,1024]{0,1:T(8,128)S(1)} %bitcast.223, f32[128,512]{1,0:T(8,128)S(1)} %fusion.81, f32[128,512]{1,0:T(8,128)S(1)} %copy-done.11, f32[128,512]{1,0:T(8,128)S(1)} %copy-done.14, f32[128,512]{1,0:T(8,128)S(1)} %copy-done.17), kind=kOutput, calls=%fused_computation.19 | convolution fusion | flops 6444285952 | bytes 9437184 | tf_op jit(solution)/shard_map/dot_general | solution.py:14
  548.8 10.3 %subtract_bitcast_fusion = f32[1,1,512,2048]{3,2,1,0:T(8,128)} fusion(f32[512,2048]{1,0:T(8,128)} %select_dynamic-update-slice_fusion, f32[512,2048]{1,0:T(8,128)S(1)} %fusion.1, f32[512,512]{1,0:T(8,128)S(1)} %bitcast.217, pred[512]{0:T(512)(128)(4,1)S(1)} %copy-done.26), kind=kOutput, calls=%fused_computation.23 | convolution fusion | flops 6443761664 | bytes 13632000 | tf_op jit(solution)/shard_map/dot_general | solution.py:14
  (280 shorter events, 215.5 us)
Async XLA Ops:
  41.4 7.6 %copy-start.23 = (f32[1,1,1024,32]{2,3,1,0:T(8,128)S(1)}, f32[1,1,1024,32]{2,3,1,0:T(8,128)}, u32[]{:S(2)}) copy-start(f32[1,1,1024,32]{2,3,1,0:T(8,128)} %param.24) | copy-start | bytes 393220
  42.1 34.0 %collective-permute-start = (f32[256,256]{0,1:T(8,128)}, f32[256,256]{0,1:T(8,128)S(1)}, u32[]{:S(2)}, u32[]{:S(2)}) collective-permute-start(f32[256,256]{0,1:T(8,128)} %slice.293), channel_id=1, source_target_pairs={{0,16},{4,20},{8,24},{12,28},{16,0},{20,4},{24,8},{28,12},{1,17},{... | collective-permute-start | bytes 786440 | tf_op jit(solution)/shard_map/ppermute | solution.py:10
  49.0 90.0 %collective-permute-start.1 = (f32[256,768]{0,1:T(8,128)S(1)}, f32[256,768]{0,1:T(8,128)}, u32[]{:S(2)}, u32[]{:S(2)}) collective-permute-start(f32[256,768]{0,1:T(8,128)S(1)} %get-tuple-element.65), channel_id=1, source_target_pairs={{0,16},{4,20},{8,24},{12,28},{16,0},{20,4},{24,8},{28,12},{1,17},{... | collective-permute-start | bytes 2359304 | tf_op jit(solution)/shard_map/ppermute | solution.py:10
  50.4 176.4 %collective-permute-start.4 = (f32[256,32]{0,1:T(8,128)}, f32[256,32]{0,1:T(8,128)}, u32[]{:S(2)}, u32[]{:S(2)}) collective-permute-start(f32[256,32]{0,1:T(8,128)} %slice_bitcast_fusion.19), channel_id=1, source_target_pairs={{0,16},{4,20},{8,24},{12,28},{16,0},{20,4},{24,8},{28,12},{1,17},{... | collective-permute-start | bytes 98312 | tf_op jit(solution)/shard_map/ppermute | solution.py:10
  65.2 72.0 %copy-start.22 = (pred[256,256]{1,0:T(32,128)(4,1)S(1)}, pred[256,256]{1,0:T(32,128)(4,1)}, u32[]{:S(2)}) copy-start(pred[256,256]{1,0:T(32,128)(4,1)} %iota_compare_fusion.2) | copy-start | bytes 196612
  144.0 7.0 %copy-start.3 = (f32[256,1536]{1,0:T(8,128)}, f32[256,1536]{1,0:T(8,128)S(1)}, u32[]{:S(2)}) copy-start(f32[256,1536]{1,0:T(8,128)S(1)} %fusion.43) | copy-start | bytes 4718596
  151.2 69.4 %collective-permute-start.2 = (f32[256,1536]{1,0:T(8,128)S(1)}, f32[256,1536]{1,0:T(8,128)S(1)}, u32[]{:S(2)}, u32[]{:S(2)}) collective-permute-start(f32[256,1536]{1,0:T(8,128)S(1)} %fusion.135), channel_id=1, source_target_pairs={{0,16},{4,20},{8,24},{12,28},{16,0},{20,4},{24,8},{28,12},{1,17},{... | collective-permute-start | bytes 4718600 | tf_op jit(solution)/shard_map/ppermute | solution.py:10
  222.7 95.0 %collective-permute-start.3 = (f32[2,256,1536]{2,1,0:T(8,128)}, f32[2,256,1536]{2,1,0:T(8,128)}, u32[]{:S(2)}, u32[]{:S(2)}) collective-permute-start(f32[2,256,1536]{2,1,0:T(8,128)} %maximum_select_fusion.2), channel_id=1, source_target_pairs={{0,2},{1,3},{2,0},{3,1},{4,6},{5,7},{6,4},{7,5},{8,10},{9,11},{10,... | collective-permute-start | bytes 9437192 | tf_op jit(solution)/shard_map/ppermute | solution.py:10
  225.4 74.8 %copy-start.31 = (pred[512]{0:T(512)(128)(4,1)}, pred[512]{0:T(512)(128)(4,1)S(1)}, u32[]{:S(2)}) copy-start(pred[512]{0:T(512)(128)(4,1)S(1)} %broadcast_in_dim.132) | copy-start | bytes 1540
  229.7 4.9 collective-permute-start.5
  234.8 58.6 %collective-permute-start.6 = (f32[2,256,32]{1,0,2:T(2,128)S(1)}, f32[2,256,32]{1,0,2:T(2,128)S(1)}, u32[]{:S(2)}, u32[]{:S(2)}) collective-permute-start(f32[2,256,32]{1,0,2:T(2,128)S(1)} %maximum_select_fusion.5), channel_id=1, source_target_pairs={{0,2},{1,3},{2,0},{3,1},{4,6},{5,7},{6,4},{7,5},{8,10},{9,11},{10,... | collective-permute-start | bytes 196616 | tf_op jit(solution)/shard_map/ppermute | solution.py:10
  516.1 6.5 %copy-start.15 = (f32[4,128,128]{1,2,0:T(8,128)}, f32[4,128,128]{1,2,0:T(8,128)S(1)}, u32[]{:S(2)}) copy-start(f32[4,128,128]{1,2,0:T(8,128)S(1)} %custom-call.44) | copy-start | bytes 786436
  539.0 8.6 %copy-start.20 = (f32[1,1,512,32]{2,3,1,0:T(8,128)S(1)}, f32[1,1,512,32]{2,3,1,0:T(8,128)}, u32[]{:S(2)}) copy-start(f32[1,1,512,32]{2,3,1,0:T(8,128)} %param.25) | copy-start | bytes 196612
  539.0 9.7 %copy-start.5 = (f32[2,64,8,256]{3,2,0,1:T(8,128)S(1)}, f32[2,64,8,256]{3,2,0,1:T(8,128)}, u32[]{:S(2)}) copy-start(f32[2,64,8,256]{3,2,0,1:T(8,128)} %copy.139) | copy-start | bytes 3145732
  539.0 9.7 %copy-start.26 = (pred[512]{0:T(512)(128)(4,1)S(1)}, pred[512]{0:T(512)(128)(4,1)}, u32[]{:S(2)}) copy-start(pred[512]{0:T(512)(128)(4,1)} %broadcast_in_dim.147) | copy-start | bytes 1540
  548.7 10.5 %collective-permute-start.7 = (f32[512,32]{0,1:T(8,128)S(1)}, f32[512,32]{0,1:T(8,128)S(1)}, u32[]{:S(2)}, u32[]{:S(2)}) collective-permute-start(f32[512,32]{0,1:T(8,128)S(1)} %fusion.8), channel_id=1, source_target_pairs={{0,16},{4,20},{8,24},{12,28},{16,0},{20,4},{24,8},{28,12},{1,17},{... | collective-permute-start | bytes 196616 | tf_op jit(solution)/shard_map/ppermute | solution.py:10
  548.8 12.2 %copy-start.24 = (f32[256,32]{0,1:T(8,128)S(1)}, f32[256,32]{0,1:T(8,128)}, u32[]{:S(2)}) copy-start(f32[256,32]{0,1:T(8,128)} %fusion.89) | copy-start | bytes 98308
  548.8 12.2 %copy-start.25 = (f32[1,1,256,32]{2,3,0,1:T(8,128)S(1)}, f32[1,1,256,32]{2,3,0,1:T(8,128)}, u32[]{:S(2)}) copy-start(f32[1,1,256,32]{2,3,0,1:T(8,128)} %copy.157) | copy-start | bytes 98308
  548.8 15.4 %copy-start.4 = (f32[256,1536]{1,0:T(8,128)S(1)}, f32[256,1536]{1,0:T(8,128)}, u32[]{:S(2)}) copy-start(f32[256,1536]{1,0:T(8,128)} %copy-done.3) | copy-start | bytes 4718596
  559.1 8.8 %copy-start.21 = (f32[2,4,8,256]{3,2,0,1:T(8,128)S(1)}, f32[2,4,8,256]{3,2,0,1:T(8,128)}, u32[]{:S(2)}) copy-start(f32[2,4,8,256]{3,2,0,1:T(8,128)} %copy.141) | copy-start | bytes 196612
  559.1 8.8 %copy-start.32 = (pred[512]{0:T(512)(128)(4,1)S(1)}, pred[512]{0:T(512)(128)(4,1)}, u32[]{:S(2)}) copy-start(pred[512]{0:T(512)(128)(4,1)} %copy-done.31) | copy-start | bytes 1540
  559.1 11.3 %copy-start.27 = (pred[4]{0:T(512)(128)(4,1)S(1)}, pred[4]{0:T(512)(128)(4,1)}, u32[]{:S(2)}) copy-start(pred[4]{0:T(512)(128)(4,1)} %get-tuple-element.49) | copy-start | bytes 16
  559.2 4.3 collective-permute-start.8
  565.0 4.9 collective-permute-start.9
  (21 other events, 50.3 us)
where the time goes:
time: 578 us; the launch traced here: 572 us
  other arithmetic  217 us (38%)
  local copies, waits for them, and re-layouts  138 us (24%)
  waiting for transfers between devices  135 us (23%)
  matrix products  59.4 us (10%)
  starting transfers between devices  13.4 us (2%)
  between operations  7.85 us (1%)
    ppermute x10, waiting for transfers between devices, partner(): return lax.ppermute(value, axis, pairs)  135 us
    another operation x21, other arithmetic, invert_spd(): factor = jnp.linalg.cholesky(matrix)  115 us
    another operation x6, other arithmetic, invert_spd(): lax.linalg.triangular_solve(factor, halfway, left_side=True, lower=True,...  63.4 us
    dot_general x10, matrix products, product(): jnp.dot(left, right, precision=lax.Precision.HIGHEST, preferred_element_t...  36.2 us
    another operation x18, local copies, waits for them, and re-layouts  17.7 us
    gather x6, local copies, waits for them, and re-layouts, pick_cols(): row_block[:, jnp.array(col_list, dtype=jnp.int32)]  15.5 us
    ppermute x10, starting transfers between devices, partner(): return lax.ppermute(value, axis, pairs)  13.4 us
  transfers between devices with their start and end apart: 10, of which 6 were waited for; matrix products, arithmetic and copies ran while one was open for 25% of the time, Pallas kernels for 0%

commit v1 on v0

v1 whole, which is shorter than its diff:
```python
import functools

import jax
import jax.numpy as jnp
from jax import lax
from jax.experimental import pallas as pl
from jax.experimental.pallas import tpu as pltpu
from jax.sharding import PartitionSpec as P

VMEM = pl.BlockSpec(memory_space=pltpu.VMEM)
SMEM = pl.BlockSpec(memory_space=pltpu.SMEM)
PARAMS = pltpu.CompilerParams(vmem_limit_bytes=60 * 2**20)

NN = (((1,), (0,)), ((), ()))
TN = (((0,), (0,)), ((), ()))
NT = (((1,), (1,)), ((), ()))


def split(value):
    high = value.astype(jnp.bfloat16)
    low = (value - high.astype(jnp.float32)).astype(jnp.bfloat16)
    return high, low


def dot_split(left, right, dims=NN):
    one = functools.partial(
        lax.dot_general, dimension_numbers=dims, preferred_element_type=jnp.float32
    )
    left_high, left_low = left
    right_high, right_low = right
    return one(left_high, right_high) + (one(left_high, right_low) + one(left_low, right_high))


def dot3(left, right, dims=NN):
    return dot_split(split(left), split(right), dims)


def dot6(left, right, dims=NN):
    return lax.dot_general(
        left,
        right,
        dims,
        precision=lax.Precision.HIGHEST,
        preferred_element_type=jnp.float32,
    )


def unit(size):
    rows = lax.broadcasted_iota(jnp.int32, (size, size), 0)
    cols = lax.broadcasted_iota(jnp.int32, (size, size), 1)
    return jnp.where(rows == cols, 1.0, 0.0).astype(jnp.float32)


def row_norm(value):
    return jnp.max(jnp.sum(jnp.abs(value), axis=1, keepdims=True))


def invert_spd(matrix_ref, out_ref, power_ref):
    size = matrix_ref.shape[0]
    matrix = matrix_ref[...]
    sums = jnp.max(jnp.sum(jnp.abs(matrix), axis=1, keepdims=True), axis=0, keepdims=True)
    scale = 1.0 / sums
    first = unit(size) - scale * matrix
    out_ref[...] = scale * (unit(size) + first)
    power_ref[...] = dot3(first, first)

    def more(state):
        count, norm = state
        return jnp.logical_and(norm > 1e-3, count < 40)

    def double(state):
        count, _ = state
        power = power_ref[...]
        parts = split(power)
        out = out_ref[...]
        out_ref[...] = out + dot_split(split(out), parts)
        square = dot_split(parts, parts)
        power_ref[...] = square
        return count + 1, row_norm(square)

    lax.while_loop(more, double, (jnp.int32(0), row_norm(power_ref[...])))

    def correct(state):
        count, _ = state
        rest = unit(size) - dot6(matrix_ref[...], out_ref[...])
        out = out_ref[...]
        out_ref[...] = out + dot3(out, rest)
        return count + 1, row_norm(rest)

    lax.while_loop(more, correct, (jnp.int32(0), jnp.float32(1.0)))


def pair_kernel(bit_ref, own_ref, other_ref, inv_ref, solve_ref, part_ref, sum_ref, power_ref, joint_ref):
    edge = own_ref.shape[0]
    bit = bit_ref[0]
    near = pl.ds(pl.multiple_of(bit * edge, edge), edge)
    far = pl.ds(pl.multiple_of((1 - bit) * edge, edge), edge)
    sum_ref[...] = own_ref[:, :edge] + other_ref[:, :edge]
    joint_ref[:, near] = own_ref[:, edge : 2 * edge]
    joint_ref[:, far] = other_ref[:, edge : 2 * edge]
    invert_spd(sum_ref, inv_ref, power_ref)
    joint = joint_ref[...]
    solve = dot6(inv_ref[...], joint)
    solve_ref[...] = solve
    part_ref[...] = -dot6(joint, solve, TN)
    part_ref[near, near] += own_ref[:, 2 * edge :]
    part_ref[far, far] += other_ref[:, 2 * edge :]


def pair_step(bit, own, other):
    edge = own.shape[0]
    shape = lambda *dims: jax.ShapeDtypeStruct(dims, jnp.float32)
    return pl.pallas_call(
        pair_kernel,
        out_shape=(shape(edge, edge), shape(edge, 2 * edge), shape(2 * edge, 2 * edge)),
        in_specs=[SMEM, VMEM, VMEM],
        out_specs=(VMEM, VMEM, VMEM),
        scratch_shapes=[
            pltpu.VMEM((edge, edge), jnp.float32),
            pltpu.VMEM((edge, edge), jnp.float32),
            pltpu.VMEM((edge, 2 * edge), jnp.float32),
        ],
        compiler_params=PARAMS,
        cost_estimate=pl.CostEstimate(
            flops=200 * edge**3, bytes_accessed=16 * edge * edge * 4, transcendentals=0
        ),
        name="pair_step",
    )(bit, own, other)


def block_kernel(own_ref, other_ref, inv_ref, lead_ref, lead_inv_ref, power_ref):
    edge = lead_ref.shape[0]
    lead_ref[...] = own_ref[:edge, :edge] + other_ref[:edge, :edge]
    invert_spd(lead_ref, lead_inv_ref, power_ref)
    lead_inv = lead_inv_ref[...]
    cross = own_ref[edge:, :edge] + other_ref[edge:, :edge]
    ratio = dot6(cross, lead_inv)
    lead_ref[...] = own_ref[edge:, edge:] + other_ref[edge:, edge:] - dot6(ratio, cross, NT)
    invert_spd(lead_ref, lead_inv_ref, power_ref)
    tail_inv = lead_inv_ref[...]
    lower = -dot6(tail_inv, ratio)
    inv_ref[edge:, edge:] = tail_inv
    inv_ref[edge:, :edge] = lower
    inv_ref[:edge, edge:] = lower.T
    inv_ref[:edge, :edge] = lead_inv - dot6(ratio, lower, TN)


def block_step(own, other):
    size = own.shape[0]
    edge = size // 2
    return pl.pallas_call(
        block_kernel,
        out_shape=jax.ShapeDtypeStruct((size, size), jnp.float32),
        in_specs=[VMEM, VMEM],
        out_specs=VMEM,
        scratch_shapes=[pltpu.VMEM((edge, edge), jnp.float32)] * 3,
        compiler_params=PARAMS,
        cost_estimate=pl.CostEstimate(
            flops=400 * edge**3, bytes_accessed=12 * edge * edge * 4, transcendentals=0
        ),
        name="block_step",
    )(own, other)


def across_kernel(bit_ref, solve_ref, sides_ref, out_ref):
    edge = solve_ref.shape[0]
    slot = pl.ds(pl.multiple_of(bit_ref[0] * edge, edge), edge)
    out_ref[...] = -dot3(solve_ref[...], sides_ref[:edge, :], TN)
    out_ref[slot, :] += sides_ref[edge:, :]


def across_step(bit, solve, sides):
    size = sides.shape[0]
    return pl.pallas_call(
        across_kernel,
        out_shape=jax.ShapeDtypeStruct((size, size), jnp.float32),
        in_specs=[SMEM, VMEM, VMEM],
        out_specs=VMEM,
        compiler_params=PARAMS,
        cost_estimate=pl.CostEstimate(
            flops=3 * size**3, bytes_accessed=10 * size * size, transcendentals=0
        ),
        name="across_step",
    )(bit, solve, sides)


def merge_kernel(
    bits_ref,
    inv_ref,
    binv_ref,
    solve_ref,
    solve_far_ref,
    kept_ref,
    sides_a_ref,
    sides_b_ref,
    across_a_ref,
    across_b_ref,
    across_c_ref,
    across_d_ref,
    data_a_ref,
    data_b_ref,
    data_c_ref,
    data_d_ref,
    map_ref,
    flux_ref,
    box_ref,
    inner_ref,
):
    edge = inv_ref.shape[0]
    two = 2 * edge
    bit_x, bit_y, side_e, side_i, side_0, side_1 = [bits_ref[index] for index in range(6)]

    def rows(slot, size):
        return pl.ds(pl.multiple_of(slot * size, size), size)

    near_x, far_x = rows(bit_x, edge), rows(1 - bit_x, edge)
    inv = inv_ref[...]
    data_a, data_b, data_c, data_d = (
        data_a_ref[...],
        data_b_ref[...],
        data_c_ref[...],
        data_d_ref[...],
    )
    binv_parts = split(binv_ref[...])
    across_a = split(across_a_ref[...])
    head = split(dot_split(across_a, binv_parts, TN))
    kept_a = sides_a_ref[:edge, :]
    kept_b = sides_b_ref[:edge, :]
    kept_a_parts = split(kept_a)
    kept_b_parts = split(kept_b)
    left = split(dot_split(kept_a_parts, split(inv), TN))

    def slot(flip_x, flip_y):
        along = 1 - bit_x if flip_x else bit_x
        up = 1 - bit_y if flip_y else bit_y
        return rows(along + 2 * up, two)

    across_b = split(across_b_ref[...])
    across_c = split(across_c_ref[...])
    across_d = split(across_d_ref[...])
    map_ref[:, slot(False, False)] = (
        kept_ref[...] - dot_split(left, kept_a_parts) - dot_split(head, across_a)
    )
    map_ref[:, slot(True, False)] = -dot_split(left, kept_b_parts) - dot_split(head, across_b)
    map_ref[:, slot(False, True)] = -dot_split(head, across_c)
    map_ref[:, slot(True, True)] = -dot_split(head, across_d)

    sum_near = data_a[:, :edge] + data_b[:, :edge]
    sum_far = data_c[:, :edge] + data_d[:, :edge]
    inner_ref[:, near_x] = data_a[:, edge:two] + data_c[:, edge:two]
    inner_ref[:, far_x] = data_b[:, edge:two] + data_d[:, edge:two]
    solve = split(solve_ref[...])
    near_parts = split(sum_near)
    block_sum = (
        inner_ref[...]
        - dot_split(near_parts, solve)
        - dot_split(split(sum_far), split(solve_far_ref[...]))
    )
    outer = [split(data[:, two : 2 * two]) for data in (data_a, data_b, data_c, data_d)]
    flux_ref[...] = (
        data_a[:, 2 * two :]
        - dot_split(near_parts, left, NT)
        - dot_split(split(block_sum), head, NT)
    ).T
    total = block_sum
    for values, across in zip(outer, (across_a, across_b, across_c, across_d)):
        total = total + dot_split(values, across, NT)
    inner = -dot_split(split(total), binv_parts)
    inner_ref[...] = inner
    pair_sum = (
        sum_near + dot_split(outer[0], kept_a_parts, NT) + dot_split(outer[1], kept_b_parts, NT)
    )
    pair_inner = -dot_split(split(pair_sum), split(inv)) - dot_split(split(inner), solve, NT)
    box_ref[rows(side_e, edge), :] = pair_inner.T
    box_ref[rows(side_i, edge), :] = inner_ref[:, near_x].T
    box_ref[rows(side_0, edge), :] = data_a[:, two : two + edge].T
    box_ref[rows(side_1, edge), :] = data_a[:, two + edge : 2 * two].T


def merge_step(*args):
    edge = args[1].shape[0]
    count = args[-1].shape[0]
    shape = lambda *dims: jax.ShapeDtypeStruct(dims, jnp.float32)
    return pl.pallas_call(
        merge_kernel,
        out_shape=(shape(2 * edge, 8 * edge), shape(2 * edge, count), shape(4 * edge, count)),
        in_specs=[SMEM] + [VMEM] * (len(args) - 1),
        out_specs=(VMEM, VMEM, VMEM),
        scratch_shapes=[pltpu.VMEM((count, 2 * edge), jnp.float32)],
        compiler_params=PARAMS,
        cost_estimate=pl.CostEstimate(
            flops=300 * edge**3, bytes_accessed=60 * edge * edge * 4, transcendentals=0
        ),
        name="merge_step",
    )(*args)


def partner(value, axis):
    count = lax.axis_size(axis)
    return lax.ppermute(value, axis, [(source, source ^ (count // 2)) for source in range(count)])


def on_device(dtn_maps, flux_part, outer_values):
    edge = dtn_maps.shape[2] // 4
    box_map, flux, outer = dtn_maps[0, 0], flux_part[0, 0], outer_values[0, 0]
    bit_x = (lax.axis_index("gx") // (lax.axis_size("gx") // 2)).astype(jnp.int32)
    bit_y = (lax.axis_index("gy") // (lax.axis_size("gy") // 2)).astype(jnp.int32)
    side_e = 1 + 2 * bit_x
    side_i = 2 - 2 * bit_y
    side_0 = bit_y * (2 - bit_x)
    side_1 = 3 - 2 * bit_x + bit_x * bit_y

    def block(row, col):
        return lax.dynamic_slice(box_map, (row * edge, col * edge), (edge, edge))

    def side(values, row):
        return lax.dynamic_slice_in_dim(values, row * edge, edge, 0)

    core = jnp.concatenate(
        [block(side_e, side_e), block(side_e, side_i), block(side_i, side_i)], axis=1
    )
    sides = jnp.concatenate(
        [
            jnp.concatenate([block(side_e, side_0), block(side_e, side_1)], axis=1),
            jnp.concatenate([block(side_i, side_0), block(side_i, side_1)], axis=1),
        ],
        axis=0,
    )
    kept = jnp.concatenate(
        [
            jnp.concatenate([block(side_0, side_0), block(side_0, side_1)], axis=1),
            jnp.concatenate([block(side_1, side_0), block(side_1, side_1)], axis=1),
        ],
        axis=0,
    )
    data = jnp.concatenate(
        [
            side(flux, side_e),
            side(flux, side_i),
            outer,
            side(flux, side_0),
            side(flux, side_1),
        ],
        axis=0,
    ).T
    shared = data[:, : 4 * edge]
    core_b = partner(core, "gx")
    core_c = partner(core, "gy")
    shared_b = partner(shared, "gx")
    sides_b = partner(sides, "gx")
    core_d = partner(core_b, "gy")
    sides_c = partner(sides, "gy")
    shared_c = partner(shared, "gy")
    shared_d = partner(shared_b, "gy")
    sides_d = partner(sides_b, "gy")

    near = bit_x[None]
    far = 1 - near
    inv, solve, part = pair_step(near, core, core_b)
    _, solve_far, part_far = pair_step(near, core_c, core_d)
    binv = block_step(part, part_far)
    across_a = across_step(near, solve, sides)
    across_c = across_step(near, solve_far, sides_c)
    across_b = across_step(far, solve, sides_b)
    across_d = across_step(far, solve_far, sides_d)
    bits = jnp.stack([bit_x, bit_y, side_e, side_i, side_0, side_1])
    merged_map, merged_flux, box_values = merge_step(
        bits,
        inv,
        binv,
        solve,
        solve_far,
        kept,
        sides,
        sides_b,
        across_a,
        across_b,
        across_c,
        across_d,
        data,
        shared_b,
        shared_c,
        shared_d,
    )
    return merged_map[None, None], merged_flux[None, None], box_values[None, None]


def solution(mesh):
    placed = P("gx", "gy", None, None)
    return jax.shard_map(
        on_device,
        mesh=mesh,
        in_specs=(placed, placed, placed),
        out_specs=(placed, placed, placed),
        check_vma=False,
    )
```

time: 578 us -> 153 us (0.26)
  other arithmetic: 217 us -> 3.29 us
  local copies, waits for them, and re-layouts: 138 us -> 9.54 us
  waiting for transfers between devices: 135 us -> 66.2 us
  Pallas kernels: 0 us -> 60.2 us
  matrix products: 59.4 us -> 0 us
  between operations: 7.85 us -> 0.8 us
    another operation x29 -> x0, other arithmetic: 180 us -> none  [the longest x21 115 us: invert_spd(): factor = jnp.linalg.cholesky(matrix)]
    ppermute x10 -> x9, waiting for transfers between devices: 135 us -> 66.2 us  [partner(): lax.ppermute(value, axis, [(source, source ^ count // 2) for source in ra...]
    pallas_call x0 -> x8, Pallas kernels: none -> 60.2 us  [the longest x2 17.6 us: pair_step(): pl.pallas_call(pair_kernel, out_shape=(shape(edge, edge), shape(edge, 2 *...]
    gather x19 -> x0, local copies, waits for them, and re-layouts: 46.3 us -> none  [the longest x6 15.5 us: pick_cols(): row_block[:, jnp.array(col_list, dtype=jnp.int32)]]
    dot_general x10 -> x0, matrix products: 36.2 us -> none  [product(): jnp.dot(left, right, precision=lax.Precision.HIGHEST, preferred_element_t...]
    another operation x37 -> x1, local copies, waits for them, and re-layouts: 32.5 us -> 0.68 us  [on_device(): bits = jnp.stack([bit_x, bit_y, side_e, side_i, side_0, side_1])]
    another operation x28 -> x0, matrix products: 23.1 us -> none  [the longest x8 9.19 us: invert_spd(): factor = jnp.linalg.cholesky(matrix)]
    slice x11 -> x1, local copies, waits for them, and re-layouts: 19.4 us -> 0.01 us  [on_device(): shared = data[:, :4 * edge]]
  transfers between devices with their start and end apart: 10 -> 9, of which waited for: 6 -> 2; matrix products, arithmetic and copies ran while one was open for 25% -> 2% of each run, Pallas kernels for 0% -> 29%
where the time goes in v1:
time: 153 us; the launch traced here: 152 us
  waiting for transfers between devices  66.2 us (43%)
  Pallas kernels  60.2 us (39%)
  starting transfers between devices  11.9 us (8%)
  local copies, waits for them, and re-layouts  9.54 us (6%)
  other arithmetic  3.29 us (2%)
    ppermute x9, waiting for transfers between devices, partner(): lax.ppermute(value, axis, [(source, source ^ count // 2) for source in ra...  66.2 us
    pallas_call x2, Pallas kernels, pair_step(): pl.pallas_call(pair_kernel, out_shape=(shape(edge, edge), shape(edge, 2 *...  17.6 us
    pallas_call x1, Pallas kernels, merge_step(): pl.pallas_call(merge_kernel, out_shape=(shape(2 * edge, 8 * edge), shape(...  16.8 us
    pallas_call x1, Pallas kernels, block_step(): pl.pallas_call(block_kernel, out_shape=jax.ShapeDtypeStruct((size, size),...  13.5 us
    pallas_call x4, Pallas kernels, across_step(): pl.pallas_call(across_kernel, out_shape=jax.ShapeDtypeStruct((size, size)...  12.3 us
    ppermute x9, starting transfers between devices, partner(): lax.ppermute(value, axis, [(source, source ^ count // 2) for source in ra...  11.9 us
    unnamed x22, local copies, waits for them, and re-layouts  5.92 us
  transfers between devices with their start and end apart: 9, of which 2 were waited for; matrix products, arithmetic and copies ran while one was open for 2% of the time, Pallas kernels for 29%

profile of v1, /device:TPU:0, one launch (start us, length us, event | category | flops | bytes accessed | tf_op | source)
XLA Modules:
  0.0 151.9 jit_solution(14787912193345261795)
XLA Ops:
  0.7 2.9 %dynamic-slice_bitcast_fusion.3 = (f32[256,256]{1,0:T(8,128)S(1)}, f32[256,256]{1,0:T(8,128)S(1)}, f32[256,256]{1,0:T(8,128)S(1)}, f32[256,256]{1,0:T(8,128)}, f...) fusion(f32[1,1,1024,1024]{3,2,1,0:T(8,128)} %param.3, ...), kind=kLoop, calls=%fused_computation.6 | loop fusion | bytes 5767184 | tf_op jit(solution)/shard_map/dynamic_slice | solution.py:314
  3.6 0.9 pad_maximum_fusion.own_ref
  4.6 4.1 %collective-permute-start = (f32[256,768]{1,0:T(8,128)}, f32[256,768]{1,0:T(8,128)}, u32[]{:S(2)}, u32[]{:S(2)}) collective-permute-start(f32[256,768]{1,0:T(8,128)} %pad_maximum_fusion.own_ref), channel_id=1, source_target_pairs={{0,16},{4,20},{8,24},{12,28},{16,0},{20,4},{24,8},{28,12},{1,17},{... | collective-permute-start | bytes 2359304 | tf_op jit(solution)/shard_map/ppermute | solution.py:300
  8.6 1.5 %collective-permute-start.1 = (f32[256,768]{1,0:T(8,128)}, f32[256,768]{1,0:T(8,128)}, u32[]{:S(2)}, u32[]{:S(2)}) collective-permute-start(f32[256,768]{1,0:T(8,128)} %pad_maximum_fusion.own_ref), channel_id=1, source_target_pairs={{0,2},{1,3},{2,0},{3,1},{4,6},{5,7},{6,4},{7,5},{8,10},{9,11},{10,... | collective-permute-start | bytes 2359304 | tf_op jit(solution)/shard_map/ppermute | solution.py:300
  10.9 55.7 %collective-permute-done.other_ref = f32[256,768]{1,0:T(8,128)} collective-permute-done((f32[256,768]{1,0:T(8,128)}, f32[256,768]{1,0:T(8,128)}, u32[]{:S(2)}, u32[]{:S(2)}) %collective-permute-start) | collective-permute-done | bytes 786464 | tf_op jit(solution)/shard_map/ppermute | solution.py:300
  66.6 1.8 %collective-permute-start.2 = (f32[256,768]{1,0:T(8,128)}, f32[256,768]{1,0:T(8,128)}, u32[]{:S(2)}, u32[]{:S(2)}) collective-permute-start(f32[256,768]{1,0:T(8,128)} %collective-permute-done.other_ref), channel_id=1, source_target_pairs={{0,2},{1,3},{2,0},{3,1},{4,6},{5,7},{6,4},{7,5},{8,10},{9,11},{10,... | collective-permute-start | bytes 2359304 | tf_op jit(solution)/shard_map/ppermute | solution.py:300
  68.5 0.7 copy-done.3
  69.3 0.7 stack.27.bits_ref
  70.0 2.2 %maximum_maximum_fusion.kept_ref = f32[512,512]{1,0:T(8,128)} fusion(f32[256,256]{1,0:T(8,128)S(1)} %get-tuple-element.24, f32[256,256]{1,0:T(8,128)} %get-tuple-element.25, f32[256,256]{1,0:T(8,128)} %get-tuple-element.26, f32[256,256]{1,0:T(8,128)} %get-tuple-element.27), kind=kLoop, calls=%fused_computation | loop fusion | flops 786432 | bytes 2097152 | tf_op jit(solution)/shard_map/concatenate | solution.py:329
  72.2 9.2 %pair_step.2 = (f32[256,256]{1,0:T(8,128)}, f32[256,512]{1,0:T(8,128)}, f32[512,512]{1,0:T(8,128)}) custom-call(s32[1]{0:T(128)} %bitcast.bit_ref, f32[256,768]{1,0:T(8,128)} %pad_maximum_fusion.own_ref, f32[256,768]{1,0:T(8,128)} %collective-permute-done.other_ref), custom_call_target="tpu_custom_call" | custom-call | flops 3355443200 | bytes 4194304 | tf_op jit(solution)/shard_map/pair_step/pallas_call | solution.py:113
  81.4 10.4 %collective-permute-done.3.sides_ref.sides_b_ref = f32[512,512]{1,0:T(8,128)S(1)} collective-permute-done((f32[512,512]{1,0:T(8,128)S(1)}, f32[512,512]{1,0:T(8,128)S(1)}, u32[]{:S(2)}, u32[]{:S(2)}) %collective-permute-start.3) | collective-permute-done | bytes 1048608 | tf_op jit(solution)/shard_map/ppermute | solution.py:300
  91.8 1.8 %collective-permute-start.5 = (f32[512,512]{1,0:T(8,128)S(1)}, f32[512,512]{1,0:T(8,128)}, u32[]{:S(2)}, u32[]{:S(2)}) collective-permute-start(f32[512,512]{1,0:T(8,128)S(1)} %collective-permute-done.3.sides_ref.sides_b_ref), channel_id=1, source_target_pairs={{0,2},{1,3},{2,0},{3,1},{4,6},{5,7},{6,4},{7,5},{8,10},{9,11},{10,... | collective-permute-start | bytes 3145736 | tf_op jit(solution)/shard_map/ppermute | solution.py:300
  93.7 3.1 %across_step.4.across_a_ref = f32[512,512]{1,0:T(8,128)} custom-call(s32[1]{0:T(128)} %bitcast.bit_ref, f32[256,512]{1,0:T(8,128)} %get-tuple-element.14.solve_ref, f32[512,512]{1,0:T(8,128)} %copy-done), custom_call_target="tpu_custom_call" | custom-call | flops 402653184 | bytes 2621440 | tf_op jit(solution)/shard_map/across_step/pallas_call | solution.py:174
  96.7 3.0 %across_step.5.across_b_ref = f32[512,512]{1,0:T(8,128)} custom-call(s32[1]{0:T(128)S(6)} %sub.24.bit_ref, f32[256,512]{1,0:T(8,128)} %get-tuple-element.14.solve_ref, f32[512,512]{1,0:T(8,128)} %copy-done.1), custom_call_target="tpu_custom_call" | custom-call | flops 402653184 | bytes 2621440 | tf_op jit(solution)/shard_map/across_step/pallas_call | solution.py:174
  100.1 1.7 %collective-permute-start.8 = (f32[32,1024]{1,0:T(8,128)}, f32[32,1024]{1,0:T(8,128)S(1)}, u32[]{:S(2)}, u32[]{:S(2)}) collective-permute-start(f32[32,1024]{1,0:T(8,128)} %collective-permute-done.6.data_b_ref), channel_id=1, source_target_pairs={{0,2},{1,3},{2,0},{3,1},{4,6},{5,7},{6,4},{7,5},{8,10},{9,11},{10,... | collective-permute-start | bytes 393224 | tf_op jit(solution)/shard_map/ppermute | solution.py:300
  101.8 8.4 %pair_step.3 = (f32[256,256]{1,0:T(8,128)}, f32[256,512]{1,0:T(8,128)}, f32[512,512]{1,0:T(8,128)}) custom-call(s32[1]{0:T(128)} %bitcast.bit_ref, f32[256,768]{1,0:T(8,128)} %collective-permute-done.1.own_ref, f32[256,768]{1,0:T(8,128)} %collective-permute-done.2.other_ref), custom_call_target="tpu_custom_call" | custom-call | flops 3355443200 | bytes 4194304 | tf_op jit(solution)/shard_map/pair_step/pallas_call | solution.py:113
  110.2 13.5 %block_step.1.binv_ref = f32[512,512]{1,0:T(8,128)} custom-call(f32[512,512]{1,0:T(8,128)} %get-tuple-element.12.own_ref, f32[512,512]{1,0:T(8,128)} %get-tuple-element.13.other_ref), custom_call_target="tpu_custom_call" | custom-call | flops 6710886400 | bytes 3145728 | tf_op jit(solution)/shard_map/block_step/pallas_call | solution.py:151
  123.7 1.0 copy-done.2
  124.7 3.0 %across_step.6.across_c_ref = f32[512,512]{1,0:T(8,128)} custom-call(s32[1]{0:T(128)} %bitcast.bit_ref, f32[256,512]{1,0:T(8,128)} %get-tuple-element.15.solve_ref.solve_far_ref, f32[512,512]{1,0:T(8,128)} %copy-done.2), custom_call_target="tpu_custom_call" | custom-call | flops 402653184 | bytes 2621440 | tf_op jit(solution)/shard_map/across_step/pallas_call | solution.py:174
  127.7 3.1 %across_step.7.across_d_ref = f32[512,512]{1,0:T(8,128)} custom-call(s32[1]{0:T(128)S(6)} %sub.24.bit_ref, f32[256,512]{1,0:T(8,128)} %get-tuple-element.15.solve_ref.solve_far_ref, f32[512,512]{1,0:T(8,128)} %collective-permute-done.5.sides_ref), custom_call_target="tpu_custom_call" | custom-call | flops 402653184 | bytes 2621440 | tf_op jit(solution)/shard_map/across_step/pallas_call | solution.py:174
  130.9 0.6 copy-done.6
  131.5 16.8 %merge_step.1 = (f32[512,2048]{1,0:T(8,128)}, f32[512,32]{1,0:T(8,128)}, f32[1024,32]{1,0:T(8,128)}) custom-call(s32[6]{0:T(128)} %stack.27.bits_ref, f32[256,256]{1,0:T(8,128)} %get-tuple-element.11.inv_ref, f32[512,512]{1,0:T(8,128)} %block_step.1.binv_ref, f32[256,512]{1,0:T(8,128)} %get-tuple-element.14.solve_ref, ...), custom_call_target="tpu_custom_call" | custom-call | flops 5033164800 | bytes 15728640 | tf_op jit(solution)/shard_map/merge_step/pallas_call | solution.py:284
  148.4 1.7 %copy.6 = f32[1,1,512,32]{2,3,1,0:T(8,128)} copy(f32[1,1,512,32]{3,2,1,0:T(8,128)} %bitcast.43) | data formatting | bytes 131072
  150.1 1.9 %copy.7 = f32[1,1,1024,32]{2,3,1,0:T(8,128)} copy(f32[1,1,1024,32]{3,2,1,0:T(8,128)} %bitcast.42) | data formatting | bytes 262144
  (31 shorter events, 1.3 us)
Async XLA Ops:
  0.7 10.2 %copy-start.4 = (f32[1,1,1024,32]{2,3,1,0:T(8,128)S(1)}, f32[1,1,1024,32]{2,3,1,0:T(8,128)}, u32[]{:S(2)}) copy-start(f32[1,1,1024,32]{2,3,1,0:T(8,128)} %param.4) | copy-start | bytes 393220
  0.7 67.8 %copy-start.5 = (f32[1,1,512,32]{2,3,1,0:T(8,128)S(1)}, f32[1,1,512,32]{2,3,1,0:T(8,128)}, u32[]{:S(2)}) copy-start(f32[1,1,512,32]{2,3,1,0:T(8,128)} %param.5) | copy-start | bytes 196612
  4.6 62.1 %collective-permute-start = (f32[256,768]{1,0:T(8,128)}, f32[256,768]{1,0:T(8,128)}, u32[]{:S(2)}, u32[]{:S(2)}) collective-permute-start(f32[256,768]{1,0:T(8,128)} %pad_maximum_fusion.own_ref), channel_id=1, source_target_pairs={{0,16},{4,20},{8,24},{12,28},{16,0},{20,4},{24,8},{28,12},{1,17},{... | collective-permute-start | bytes 2359304 | tf_op jit(solution)/shard_map/ppermute | solution.py:300
  8.6 91.5 %collective-permute-start.1 = (f32[256,768]{1,0:T(8,128)}, f32[256,768]{1,0:T(8,128)}, u32[]{:S(2)}, u32[]{:S(2)}) collective-permute-start(f32[256,768]{1,0:T(8,128)} %pad_maximum_fusion.own_ref), channel_id=1, source_target_pairs={{0,2},{1,3},{2,0},{3,1},{4,6},{5,7},{6,4},{7,5},{8,10},{9,11},{10,... | collective-permute-start | bytes 2359304 | tf_op jit(solution)/shard_map/ppermute | solution.py:300
  10.3 71.1 %copy-start = (f32[512,512]{1,0:T(8,128)}, f32[512,512]{1,0:T(8,128)S(1)}, u32[]{:S(2)}) copy-start(f32[512,512]{1,0:T(8,128)S(1)} %maximum_maximum_fusion.1.sides_ref.sides_a_ref) | copy-start | bytes 3145732
  10.3 113.4 %collective-permute-start.4 = (f32[512,512]{1,0:T(8,128)S(1)}, f32[512,512]{1,0:T(8,128)S(1)}, u32[]{:S(2)}, u32[]{:S(2)}) collective-permute-start(f32[512,512]{1,0:T(8,128)S(1)} %maximum_maximum_fusion.1.sides_ref.sides_a_ref), channel_id=1, source_target_pairs={{0,2},{1,3},{2,0},{3,1},{4,6},{5,7},{6,4},{7,5},{8,10},{9,11},{10,... | collective-permute-start | bytes 3145736 | tf_op jit(solution)/shard_map/ppermute | solution.py:300
  10.9 81.0 %collective-permute-start.3 = (f32[512,512]{1,0:T(8,128)S(1)}, f32[512,512]{1,0:T(8,128)S(1)}, u32[]{:S(2)}, u32[]{:S(2)}) collective-permute-start(f32[512,512]{1,0:T(8,128)S(1)} %maximum_maximum_fusion.1.sides_ref.sides_a_ref), channel_id=1, source_target_pairs={{0,16},{4,20},{8,24},{12,28},{16,0},{20,4},{24,8},{28,12},{1,17},{... | collective-permute-start | bytes 3145736 | tf_op jit(solution)/shard_map/ppermute | solution.py:300
  66.6 35.2 %collective-permute-start.2 = (f32[256,768]{1,0:T(8,128)}, f32[256,768]{1,0:T(8,128)}, u32[]{:S(2)}, u32[]{:S(2)}) collective-permute-start(f32[256,768]{1,0:T(8,128)} %collective-permute-done.other_ref), channel_id=1, source_target_pairs={{0,2},{1,3},{2,0},{3,1},{4,6},{5,7},{6,4},{7,5},{8,10},{9,11},{10,... | collective-permute-start | bytes 2359304 | tf_op jit(solution)/shard_map/ppermute | solution.py:300
  68.5 0.7 copy-start.3
  69.2 30.6 %collective-permute-start.6 = (f32[32,1024]{1,0:T(8,128)S(1)}, f32[32,1024]{1,0:T(8,128)}, u32[]{:S(2)}, u32[]{:S(2)}) collective-permute-start(f32[32,1024]{1,0:T(8,128)S(1)} %slice.4), channel_id=1, source_target_pairs={{0,16},{4,20},{8,24},{12,28},{16,0},{20,4},{24,8},{28,12},{1,17},{... | collective-permute-start | bytes 393224 | tf_op jit(solution)/shard_map/ppermute | solution.py:300
  91.8 4.9 %copy-start.1 = (f32[512,512]{1,0:T(8,128)}, f32[512,512]{1,0:T(8,128)S(1)}, u32[]{:S(2)}) copy-start(f32[512,512]{1,0:T(8,128)S(1)} %collective-permute-done.3.sides_ref.sides_b_ref) | copy-start | bytes 3145732
  91.8 35.9 %collective-permute-start.5 = (f32[512,512]{1,0:T(8,128)S(1)}, f32[512,512]{1,0:T(8,128)}, u32[]{:S(2)}, u32[]{:S(2)}) collective-permute-start(f32[512,512]{1,0:T(8,128)S(1)} %collective-permute-done.3.sides_ref.sides_b_ref), channel_id=1, source_target_pairs={{0,2},{1,3},{2,0},{3,1},{4,6},{5,7},{6,4},{7,5},{8,10},{9,11},{10,... | collective-permute-start | bytes 3145736 | tf_op jit(solution)/shard_map/ppermute | solution.py:300
  99.8 31.1 %collective-permute-start.7 = (f32[32,1024]{1,0:T(8,128)S(1)}, f32[32,1024]{1,0:T(8,128)S(1)}, u32[]{:S(2)}, u32[]{:S(2)}) collective-permute-start(f32[32,1024]{1,0:T(8,128)S(1)} %slice.4), channel_id=1, source_target_pairs={{0,2},{1,3},{2,0},{3,1},{4,6},{5,7},{6,4},{7,5},{8,10},{9,11},{10,... | collective-permute-start | bytes 393224 | tf_op jit(solution)/shard_map/ppermute | solution.py:300
  100.1 30.7 %collective-permute-start.8 = (f32[32,1024]{1,0:T(8,128)}, f32[32,1024]{1,0:T(8,128)S(1)}, u32[]{:S(2)}, u32[]{:S(2)}) collective-permute-start(f32[32,1024]{1,0:T(8,128)} %collective-permute-done.6.data_b_ref), channel_id=1, source_target_pairs={{0,2},{1,3},{2,0},{3,1},{4,6},{5,7},{6,4},{7,5},{8,10},{9,11},{10,... | collective-permute-start | bytes 393224 | tf_op jit(solution)/shard_map/ppermute | solution.py:300
  123.7 1.0 copy-start.2
  130.8 0.7 copy-start.6
  130.9 0.7 copy-start.7

commit v2 on v1

v2 whole, which is shorter than its diff:
```python
import functools

import jax
import jax.numpy as jnp
from jax import lax
from jax.experimental import pallas as pl
from jax.experimental.pallas import tpu as pltpu
from jax.sharding import PartitionSpec as P

VMEM = pl.BlockSpec(memory_space=pltpu.VMEM)
SMEM = pl.BlockSpec(memory_space=pltpu.SMEM)
PARAMS = pltpu.CompilerParams(vmem_limit_bytes=60 * 2**20)

NN = (((1,), (0,)), ((), ()))
TN = (((0,), (0,)), ((), ()))
NT = (((1,), (1,)), ((), ()))


def split(value):
    high = value.astype(jnp.bfloat16)
    low = (value - high.astype(jnp.float32)).astype(jnp.bfloat16)
    return high, low


def dot_split(left, right, dims=NN):
    one = functools.partial(
        lax.dot_general, dimension_numbers=dims, preferred_element_type=jnp.float32
    )
    left_high, left_low = left
    right_high, right_low = right
    return one(left_high, right_high) + (one(left_high, right_low) + one(left_low, right_high))


def dot3(left, right, dims=NN):
    return dot_split(split(left), split(right), dims)


def dot6(left, right, dims=NN):
    return lax.dot_general(
        left,
        right,
        dims,
        precision=lax.Precision.HIGHEST,
        preferred_element_type=jnp.float32,
    )


def unit(size):
    rows = lax.broadcasted_iota(jnp.int32, (size, size), 0)
    cols = lax.broadcasted_iota(jnp.int32, (size, size), 1)
    return jnp.where(rows == cols, 1.0, 0.0).astype(jnp.float32)


def row_norm(value):
    return jnp.max(jnp.sum(jnp.abs(value), axis=1, keepdims=True))


def invert_spd(matrix_ref, out_ref, power_ref):
    size = matrix_ref.shape[0]
    matrix = matrix_ref[...]
    sums = jnp.max(jnp.sum(jnp.abs(matrix), axis=1, keepdims=True), axis=0, keepdims=True)
    scale = 1.0 / sums
    first = unit(size) - scale * matrix
    out_ref[...] = scale * (unit(size) + first)
    power_ref[...] = dot3(first, first)

    def more(state):
        count, norm = state
        return jnp.logical_and(norm > 1e-3, count < 40)

    def double(state):
        count, _ = state
        power = power_ref[...]
        parts = split(power)
        out = out_ref[...]
        out_ref[...] = out + dot_split(split(out), parts)
        square = dot_split(parts, parts)
        power_ref[...] = square
        return count + 1, row_norm(square)

    lax.while_loop(more, double, (jnp.int32(0), row_norm(power_ref[...])))

    def correct(state):
        count, _ = state
        rest = unit(size) - dot6(matrix_ref[...], out_ref[...])
        out = out_ref[...]
        out_ref[...] = out + dot3(out, rest)
        return count + 1, row_norm(rest)

    lax.while_loop(more, correct, (jnp.int32(0), jnp.float32(1.0)))


def unpack(core_ref, index):
    half = core_ref.shape[0]
    base = 3 * half * index
    lead = core_ref[:, base : base + half]
    cross = core_ref[:, base + half : base + 2 * half]
    tail = core_ref[:, base + 2 * half : base + 3 * half]
    return jnp.concatenate(
        [
            jnp.concatenate([lead, cross], axis=1),
            jnp.concatenate([cross.T, tail], axis=1),
        ],
        axis=0,
    )


def pair_kernel(bit_ref, own_ref, other_ref, inv_ref, solve_ref, part_ref, sum_ref, power_ref, joint_ref):
    half = own_ref.shape[0]
    edge = 2 * half
    bit = bit_ref[0]
    near = pl.ds(pl.multiple_of(bit * edge, edge), edge)
    far = pl.ds(pl.multiple_of((1 - bit) * edge, edge), edge)
    sum_ref[...] = unpack(own_ref, 0) + unpack(other_ref, 0)
    for place, ref in ((near, own_ref), (far, other_ref)):
        joint_ref[:half, place] = ref[:, 3 * edge : 4 * edge]
        joint_ref[half:, place] = ref[:, 4 * edge : 5 * edge]
    invert_spd(sum_ref, inv_ref, power_ref)
    joint = joint_ref[...]
    solve = dot6(inv_ref[...], joint)
    solve_ref[...] = solve
    part_ref[...] = -dot6(joint, solve, TN)
    part_ref[near, near] += unpack(own_ref, 1)
    part_ref[far, far] += unpack(other_ref, 1)


def pair_step(bit, own, other):
    edge = 2 * own.shape[0]
    shape = lambda *dims: jax.ShapeDtypeStruct(dims, jnp.float32)
    return pl.pallas_call(
        pair_kernel,
        out_shape=(shape(edge, edge), shape(edge, 2 * edge), shape(2 * edge, 2 * edge)),
        in_specs=[SMEM, VMEM, VMEM],
        out_specs=(VMEM, VMEM, VMEM),
        scratch_shapes=[
            pltpu.VMEM((edge, edge), jnp.float32),
            pltpu.VMEM((edge, edge), jnp.float32),
            pltpu.VMEM((edge, 2 * edge), jnp.float32),
        ],
        compiler_params=PARAMS,
        cost_estimate=pl.CostEstimate(
            flops=200 * edge**3, bytes_accessed=16 * edge * edge * 4, transcendentals=0
        ),
        name="pair_step",
    )(bit, own, other)


def block_kernel(
    bit_ref,
    own_ref,
    other_ref,
    pair_inv_ref,
    solve_ref,
    solve_far_ref,
    sides_ref,
    inv_ref,
    head_ref,
    left_ref,
    near_ref,
    far_ref,
    lead_ref,
    lead_inv_ref,
    power_ref,
    across_ref,
):
    edge = lead_ref.shape[0]
    lead_ref[...] = own_ref[:edge, :edge] + other_ref[:edge, :edge]
    invert_spd(lead_ref, lead_inv_ref, power_ref)
    lead_inv = lead_inv_ref[...]
    cross = own_ref[edge:, :edge] + other_ref[edge:, :edge]
    ratio = dot6(cross, lead_inv)
    lead_ref[...] = own_ref[edge:, edge:] + other_ref[edge:, edge:] - dot6(ratio, cross, NT)
    invert_spd(lead_ref, lead_inv_ref, power_ref)
    tail_inv = lead_inv_ref[...]
    lower = -dot6(tail_inv, ratio)
    inv_ref[edge:, edge:] = tail_inv
    inv_ref[edge:, :edge] = lower
    inv_ref[:edge, edge:] = lower.T
    inv_ref[:edge, :edge] = lead_inv - dot6(ratio, lower, TN)

    slot = pl.ds(pl.multiple_of(bit_ref[0] * edge, edge), edge)
    solve = split(solve_ref[...])
    kept = split(sides_ref[:edge, :])
    across_ref[...] = -dot_split(solve, kept, TN)
    across_ref[slot, :] += sides_ref[edge:, :]
    head = dot3(across_ref[...], inv_ref[...], TN)
    head_ref[...] = head
    head = split(head)
    left = dot_split(kept, split(pair_inv_ref[...]), TN)
    left_ref[...] = left
    near_ref[...] = left - dot_split(head, solve, NT)
    far_ref[...] = -dot_split(head, split(solve_far_ref[...]), NT)


def block_step(bit, own, *rest):
    size = own.shape[0]
    edge = size // 2
    shape = lambda *dims: jax.ShapeDtypeStruct(dims, jnp.float32)
    return pl.pallas_call(
        block_kernel,
        out_shape=(shape(size, size), shape(size, size)) + (shape(size, edge),) * 3,
        in_specs=[SMEM] + [VMEM] * 6,
        out_specs=(VMEM,) * 5,
        scratch_shapes=[pltpu.VMEM((edge, edge), jnp.float32)] * 3
        + [pltpu.VMEM((size, size), jnp.float32)],
        compiler_params=PARAMS,
        cost_estimate=pl.CostEstimate(
            flops=600 * edge**3, bytes_accessed=30 * edge * edge * 4, transcendentals=0
        ),
        name="block_step",
    )(bit, own, *rest)


def merge_kernel(
    bits_ref,
    inv_ref,
    binv_ref,
    head_ref,
    left_ref,
    near_ref,
    far_ref,
    solve_ref,
    solve_far_ref,
    kept_ref,
    sides_a_ref,
    sides_b0_ref,
    sides_b1_ref,
    sides_c_ref,
    sides_d0_ref,
    sides_d1_ref,
    data_a_ref,
    data_b_ref,
    data_c_ref,
    data_d_ref,
    map_ref,
    flux_ref,
    box_ref,
    inner_ref,
    work_ref,
    sems,
):
    edge = inv_ref.shape[0]
    two = 2 * edge
    bit_x, bit_y, side_e, side_i, side_0, side_1 = [bits_ref[index] for index in range(6)]

    def rows(slot, size):
        return pl.ds(pl.multiple_of(slot * size, size), size)

    near_x, far_x = rows(bit_x, edge), rows(1 - bit_x, edge)
    near = split(near_ref[...])
    far = split(far_ref[...])
    head_near = split(head_ref[:, near_x])
    head_far = split(head_ref[:, far_x])
    copies = []

    def put(index, along, up, lead, tail, pieces, base=None):
        for count, (top, low) in enumerate(pieces):
            part = slice(index * two + count * edge, index * two + (count + 1) * edge)
            value = -dot_split(lead, top) - dot_split(tail, low)
            if base is not None:
                value = value + base[:, count * edge : (count + 1) * edge]
            work_ref[:, part] = value
        copy = pltpu.make_async_copy(
            work_ref.at[:, pl.ds(index * two, two)],
            map_ref.at[:, rows(along + 2 * up, two)],
            sems.at[index],
        )
        copy.start()
        copies.append(copy)

    def whole(ref):
        return [
            (split(ref[:edge, :edge]), split(ref[edge:, :edge])),
            (split(ref[:edge, edge:]), split(ref[edge:, edge:])),
        ]

    def halves(*refs):
        return [(split(ref[:edge, :]), split(ref[edge:, :])) for ref in refs]

    side_a = whole(sides_a_ref)
    side_b = halves(sides_b0_ref, sides_b1_ref)
    side_c = whole(sides_c_ref)
    side_d = halves(sides_d0_ref, sides_d1_ref)
    put(0, bit_x, bit_y, near, head_near, side_a, kept_ref[...])
    put(1, 1 - bit_x, bit_y, near, head_far, side_b)
    put(2, bit_x, 1 - bit_y, far, head_near, side_c)
    put(3, 1 - bit_x, 1 - bit_y, far, head_far, side_d)

    refs = (data_a_ref, data_b_ref, data_c_ref, data_d_ref)
    sum_near = data_a_ref[:, :edge] + data_b_ref[:, :edge]
    sum_far = data_c_ref[:, :edge] + data_d_ref[:, :edge]
    top = []
    low = []
    for ref, side in zip(refs, (side_a, side_b, side_c, side_d)):
        values = [split(ref[:, two + count * edge : two + (count + 1) * edge]) for count in (0, 1)]
        top.append(sum(dot_split(value, piece[0], NT) for value, piece in zip(values, side)))
        low.append(sum(dot_split(value, piece[1], NT) for value, piece in zip(values, side)))
    inv = split(inv_ref[...])
    solve = split(solve_ref[...])
    solve_far = split(solve_far_ref[...])
    inner_ref[:, near_x] = data_a_ref[:, edge:two] + data_c_ref[:, edge:two]
    inner_ref[:, far_x] = data_b_ref[:, edge:two] + data_d_ref[:, edge:two]
    near_sum = split(sum_near)
    block_sum = (
        inner_ref[...] - dot_split(near_sum, solve) - dot_split(split(sum_far), solve_far)
    )
    flux_ref[...] = (
        data_a_ref[:, 2 * two :]
        - dot_split(near_sum, split(left_ref[...]), NT)
        - dot_split(split(block_sum), split(head_ref[...]), NT)
    )
    pair_near = top[0] + top[1]
    inner_ref[:, near_x] = low[0] + low[2]
    inner_ref[:, far_x] = low[1] + low[3]
    total = (
        block_sum
        + inner_ref[...]
        - dot_split(split(pair_near), solve)
        - dot_split(split(top[2] + top[3]), solve_far)
    )
    inner = -dot_split(split(total), split(binv_ref[...]))
    inner_ref[...] = inner
    pair_inner = -dot_split(split(sum_near + pair_near), inv) - dot_split(split(inner), solve, NT)
    box_ref[:, rows(side_e, edge)] = pair_inner
    box_ref[:, rows(side_i, edge)] = inner_ref[:, near_x]
    box_ref[:, rows(side_0, edge)] = data_a_ref[:, two : two + edge]
    box_ref[:, rows(side_1, edge)] = data_a_ref[:, two + edge : 2 * two]
    for copy in copies:
        copy.wait()


def merge_step(*args):
    edge = args[1].shape[0]
    count = args[-1].shape[0]
    shape = lambda *dims: jax.ShapeDtypeStruct(dims, jnp.float32)
    return pl.pallas_call(
        merge_kernel,
        out_shape=(shape(2 * edge, 8 * edge), shape(count, 2 * edge), shape(count, 4 * edge)),
        in_specs=[SMEM] + [VMEM] * (len(args) - 1),
        out_specs=(pl.BlockSpec(memory_space=pl.ANY), VMEM, VMEM),
        scratch_shapes=[
            pltpu.VMEM((count, 2 * edge), jnp.float32),
            pltpu.VMEM((2 * edge, 8 * edge), jnp.float32),
            pltpu.SemaphoreType.DMA((4,)),
        ],
        compiler_params=PARAMS,
        cost_estimate=pl.CostEstimate(
            flops=300 * edge**3, bytes_accessed=60 * edge * edge * 4, transcendentals=0
        ),
        name="merge_step",
    )(*args)


def partner(value, axis):
    count = lax.axis_size(axis)
    return lax.ppermute(value, axis, [(source, source ^ (count // 2)) for source in range(count)])


def on_device(dtn_maps, flux_part, outer_values):
    edge = dtn_maps.shape[2] // 4
    box_map, flux, outer = dtn_maps[0, 0], flux_part[0, 0], outer_values[0, 0]
    bit_x = (lax.axis_index("gx") // (lax.axis_size("gx") // 2)).astype(jnp.int32)
    bit_y = (lax.axis_index("gy") // (lax.axis_size("gy") // 2)).astype(jnp.int32)
    side_e = 1 + 2 * bit_x
    side_i = 2 - 2 * bit_y
    side_0 = bit_y * (2 - bit_x)
    side_1 = 3 - 2 * bit_x + bit_x * bit_y

    def block(row, col):
        return lax.dynamic_slice(box_map, (row * edge, col * edge), (edge, edge))

    def side(values, row):
        return lax.dynamic_slice_in_dim(values, row * edge, edge, 0)

    half = edge // 2

    def halves(row, col, across, down):
        start = (row * edge + across * half, col * edge + down * half)
        return lax.dynamic_slice(box_map, start, (half, half))

    def packed(row):
        return [halves(row, row, 0, 0), halves(row, row, 0, 1), halves(row, row, 1, 1)]

    def strip(number):
        start = (side_e * edge + number * half, side_i * edge)
        return lax.dynamic_slice(box_map, start, (half, edge))

    core = jnp.concatenate(packed(side_e) + packed(side_i) + [strip(0), strip(1)], axis=1)
    sides_0 = jnp.concatenate([block(side_e, side_0), block(side_i, side_0)], axis=0)
    sides_1 = jnp.concatenate([block(side_e, side_1), block(side_i, side_1)], axis=0)
    sides = jnp.concatenate([sides_0, sides_1], axis=1)
    kept = jnp.concatenate(
        [
            jnp.concatenate([block(side_0, side_0), block(side_0, side_1)], axis=1),
            jnp.concatenate([block(side_1, side_0), block(side_1, side_1)], axis=1),
        ],
        axis=0,
    )
    data = jnp.concatenate(
        [
            side(flux, side_e),
            side(flux, side_i),
            outer,
            side(flux, side_0),
            side(flux, side_1),
        ],
        axis=0,
    ).T
    shared = data[:, : 4 * edge]
    core_b = partner(core, "gx")
    core_c = partner(core, "gy")
    sides_c = partner(sides, "gy")
    shared_c = partner(shared, "gy")
    sides_0, core_b, core_c, sides_c, shared_c = lax.optimization_barrier(
        (sides_0, core_b, core_c, sides_c, shared_c)
    )
    core_d = partner(core_b, "gy")
    sides_b0 = partner(sides_0, "gx")
    shared_b = partner(shared, "gx")

    near = bit_x[None]
    inv, solve, part = pair_step(near, core, core_b)
    _, solve_far, part_far = pair_step(near, core_c, core_d)
    sides_1, sides_b0, part, part_far, shared_b = lax.optimization_barrier(
        (sides_1, sides_b0, part, part_far, shared_b)
    )
    sides_b1 = partner(sides_1, "gx")
    shared_d = partner(shared_b, "gy")
    sides_d0 = partner(sides_b0, "gy")
    sides_d1 = partner(sides_b1, "gy")

    binv, head, left, lead_near, lead_far = block_step(
        near, part, part_far, inv, solve, solve_far, sides
    )
    bits = jnp.stack([bit_x, bit_y, side_e, side_i, side_0, side_1])
    merged_map, merged_flux, box_values = merge_step(
        bits,
        inv,
        binv,
        head,
        left,
        lead_near,
        lead_far,
        solve,
        solve_far,
        kept,
        sides,
        sides_b0,
        sides_b1,
        sides_c,
        sides_d0,
        sides_d1,
        data,
        shared_b,
        shared_c,
        shared_d,
    )
    merged_flux, box_values = merged_flux.T, box_values.T
    return merged_map[None, None], merged_flux[None, None], box_values[None, None]


def solution(mesh):
    placed = P("gx", "gy", None, None)
    return jax.shard_map(
        on_device,
        mesh=mesh,
        in_specs=(placed, placed, placed),
        out_specs=(placed, placed, placed),
        check_vma=False,
    )
```

time: 153 us -> 137 us (0.90)
  Pallas kernels: 60.2 us -> 46.1 us
  waiting for transfers between devices: 66.2 us -> 57.5 us
  local copies, waits for them, and re-layouts: 9.54 us -> 15.7 us
  starting transfers between devices: 11.9 us -> 14.7 us
  other arithmetic: 3.29 us -> 1.37 us
    ppermute x9 -> x11, waiting for transfers between devices: 66.2 us -> 57.5 us  [partner(): lax.ppermute(value, axis, [(source, source ^ count // 2) for source in ra...]
    pallas_call x5 -> x1, Pallas kernels: 25.8 us -> 17.4 us  [block_step(): pl.pallas_call(block_kernel, out_shape=(shape(size, size), shape(size, si...]
    unnamed x22 -> x33, local copies, waits for them, and re-layouts: 5.92 us -> 11.5 us
    pallas_call x1, Pallas kernels: 16.8 us -> 11.9 us  [merge_step(): pl.pallas_call(merge_kernel, out_shape=(shape(2 * edge, 8 * edge), shape(...]
    ppermute x9 -> x11, starting transfers between devices: 11.9 us -> 14.7 us  [partner(): lax.ppermute(value, axis, [(source, source ^ count // 2) for source in ra...]
    concatenate x0 -> x1, local copies, waits for them, and re-layouts: none -> 1.6 us  [on_device(): jnp.concatenate(packed(side_e) + packed(side_i) + [strip(0), strip(1)], a...]
  transfers between devices with their start and end apart: 9 -> 11, of which waited for: 2 -> 5; matrix products, arithmetic and copies ran while one was open for 2% -> 10% of each run, Pallas kernels for 29% -> 25%
where the time goes in v2:
time: 137 us; the launch traced here: 136 us
  waiting for transfers between devices  57.5 us (42%)
  Pallas kernels  46.1 us (34%)
  local copies, waits for them, and re-layouts  15.7 us (11%)
  starting transfers between devices  14.7 us (11%)
  other arithmetic  1.37 us (1%)
    ppermute x11, waiting for transfers between devices, partner(): lax.ppermute(value, axis, [(source, source ^ count // 2) for source in ra...  57.5 us
    pallas_call x1, Pallas kernels, block_step(): pl.pallas_call(block_kernel, out_shape=(shape(size, size), shape(size, si...  17.4 us
    pallas_call x2, Pallas kernels, pair_step(): pl.pallas_call(pair_kernel, out_shape=(shape(edge, edge), shape(edge, 2 *...  16.8 us
    ppermute x11, starting transfers between devices, partner(): lax.ppermute(value, axis, [(source, source ^ count // 2) for source in ra...  14.7 us
    pallas_call x1, Pallas kernels, merge_step(): pl.pallas_call(merge_kernel, out_shape=(shape(2 * edge, 8 * edge), shape(...  11.9 us
    unnamed x33, local copies, waits for them, and re-layouts  11.5 us
  transfers between devices with their start and end apart: 11, of which 5 were waited for; matrix products, arithmetic and copies ran while one was open for 10% of the time, Pallas kernels for 25%

profile of v2, /device:TPU:0, one launch (start us, length us, event | category | flops | bytes accessed | tf_op | source)
XLA Modules:
  0.0 136.4 jit_solution(16226379291442239938)
XLA Ops:
  0.7 1.8 %dynamic-slice_bitcast_fusion.3 = (f32[256,256]{1,0:T(8,128)S(1)}, f32[256,256]{1,0:T(8,128)S(1)}, f32[256,256]{1,0:T(8,128)S(1)}, f32[256,256]{1,0:T(8,128)S(1)...) fusion(f32[1,1,1024,1024]{3,2,1,0:T(8,128)} %param.3, ...), kind=kLoop, calls=%fused_computation.7 | loop fusion | bytes 4194320 | tf_op jit(solution)/shard_map/dynamic_slice | solution.py:370
  2.7 3.1 %collective-permute-start.2 = (f32[512,512]{1,0:T(8,128)S(1)}, f32[512,512]{1,0:T(8,128)}, u32[]{:S(2)}, u32[]{:S(2)}) collective-permute-start(f32[512,512]{1,0:T(8,128)S(1)} %maximum_maximum_fusion.sides_ref.sides_a_ref), channel_id=1, source_target_pairs={{0,2},{1,3},{2,0},{3,1},{4,6},{5,7},{6,4},{7,5},{8,10},{9,11},{10,... | collective-permute-start | bytes 3145736 | tf_op jit(solution)/shard_map/ppermute | solution.py:356
  5.7 1.5 %bitcast_dynamic-update-slice_fusion.8 = f32[128,1280]{1,0:T(8,128)} fusion(f32[1,1,1024,1024]{3,2,1,0:T(8,128)} %param.3, s32[]{:T(128)S(6)} %select_n.22), kind=kLoop, calls=%fused_computation.20 | loop fusion | bytes 131076
  7.2 1.5 %bitcast_dynamic-update-slice_fusion.7 = f32[128,1280]{1,0:T(8,128)} fusion(f32[128,1280]{1,0:T(8,128)} %bitcast_dynamic-update-slice_fusion.8, f32[1,1,1024,1024]{3,2,1,0:T(8,128)} %param.3, s32[]{:T(128)S(6)} %select_n.22, s32[]{:T(128)S(6)} %select_n.23), kind=kLoop, calls=%fused_computation.19 | loop fusion | bytes 131080
  8.7 1.5 %bitcast_dynamic-update-slice_fusion.6 = f32[128,1280]{1,0:T(8,128)} fusion(f32[128,1280]{1,0:T(8,128)} %bitcast_dynamic-update-slice_fusion.7, f32[1,1,1024,1024]{3,2,1,0:T(8,128)} %param.3, s32[]{:T(128)S(6)} %select_n.23), kind=kLoop, calls=%fused_computation.18 | loop fusion | bytes 131076
  10.2 1.5 %bitcast_dynamic-update-slice_fusion.5 = f32[128,1280]{1,0:T(8,128)} fusion(f32[128,1280]{1,0:T(8,128)} %bitcast_dynamic-update-slice_fusion.6, f32[1,1,1024,1024]{3,2,1,0:T(8,128)} %param.3, s32[]{:T(128)S(6)} %select_n.24), kind=kLoop, calls=%fused_computation.17 | loop fusion | bytes 131076
  11.6 1.5 %bitcast_dynamic-update-slice_fusion.4 = f32[128,1280]{1,0:T(8,128)} fusion(f32[128,1280]{1,0:T(8,128)} %bitcast_dynamic-update-slice_fusion.5, f32[1,1,1024,1024]{3,2,1,0:T(8,128)} %param.3, s32[]{:T(128)S(6)} %select_n.24, s32[]{:T(128)S(6)} %select_n.25), kind=kLoop, calls=%fused_computation.16 | loop fusion | bytes 131080
  13.1 1.5 %bitcast_dynamic-update-slice_fusion.3 = f32[128,1280]{1,0:T(8,128)} fusion(f32[128,1280]{1,0:T(8,128)} %bitcast_dynamic-update-slice_fusion.4, f32[1,1,1024,1024]{3,2,1,0:T(8,128)} %param.3, s32[]{:T(128)S(6)} %select_n.25), kind=kLoop, calls=%fused_computation.15 | loop fusion | bytes 131076
  14.6 1.6 %bitcast_dynamic-update-slice_fusion.1 = f32[128,1280]{1,0:T(8,128)} fusion(f32[128,1280]{1,0:T(8,128)} %bitcast_dynamic-update-slice_fusion.3, f32[1,1,1024,1024]{3,2,1,0:T(8,128)} %param.3, s32[]{:T(128)S(6)} %select_n.22, s32[]{:T(128)S(6)} %select_n.24), kind=kLoop, calls=%fused_computation.13 | loop fusion | bytes 262152
  16.2 1.6 %bitcast_dynamic-update-slice_fusion.own_ref = f32[128,1280]{1,0:T(8,128)} fusion(f32[128,1280]{1,0:T(8,128)} %bitcast_dynamic-update-slice_fusion.1, f32[1,1,1024,1024]{3,2,1,0:T(8,128)} %param.3, s32[]{:T(128)S(6)} %select_n.23, s32[]{:T(128)S(6)} %select_n.24), kind=kLoop, calls=%fused_computation.12 | loop fusion | bytes 262152 | tf_op jit(solution)/shard_map/concatenate | solution.py:388
  17.9 3.0 %collective-permute-start = (f32[128,1280]{1,0:T(8,128)}, f32[128,1280]{1,0:T(8,128)}, u32[]{:S(2)}, u32[]{:S(2)}) collective-permute-start(f32[128,1280]{1,0:T(8,128)} %bitcast_dynamic-update-slice_fusion.own_ref), channel_id=1, source_target_pairs={{0,16},{4,20},{8,24},{12,28},{16,0},{20,4},{24,8},{28,12},{1,17},{... | collective-permute-start | bytes 1966088 | tf_op jit(solution)/shard_map/ppermute | solution.py:356
  21.0 1.6 %collective-permute-start.3 = (f32[32,1024]{1,0:T(8,128)S(1)}, f32[32,1024]{1,0:T(8,128)S(1)}, u32[]{:S(2)}, u32[]{:S(2)}) collective-permute-start(f32[32,1024]{1,0:T(8,128)S(1)} %slice.4), channel_id=1, source_target_pairs={{0,2},{1,3},{2,0},{3,1},{4,6},{5,7},{6,4},{7,5},{8,10},{9,11},{10,... | collective-permute-start | bytes 393224 | tf_op jit(solution)/shard_map/ppermute | solution.py:356
  22.6 23.1 %collective-permute-done.3.data_c_ref = f32[32,1024]{1,0:T(8,128)S(1)} collective-permute-done((f32[32,1024]{1,0:T(8,128)S(1)}, f32[32,1024]{1,0:T(8,128)S(1)}, u32[]{:S(2)}, u32[]{:S(2)}) %collective-permute-start.3) | collective-permute-done | bytes 131104 | tf_op jit(solution)/shard_map/ppermute | solution.py:356
  45.7 3.8 %collective-permute-done.other_ref = f32[128,1280]{1,0:T(8,128)} collective-permute-done((f32[128,1280]{1,0:T(8,128)}, f32[128,1280]{1,0:T(8,128)}, u32[]{:S(2)}, u32[]{:S(2)}) %collective-permute-start) | collective-permute-done | bytes 655392 | tf_op jit(solution)/shard_map/ppermute | solution.py:356
  49.5 1.5 %collective-permute-start.5 = (f32[128,1280]{1,0:T(8,128)}, f32[128,1280]{1,0:T(8,128)}, u32[]{:S(2)}, u32[]{:S(2)}) collective-permute-start(f32[128,1280]{1,0:T(8,128)} %collective-permute-done.other_ref), channel_id=1, source_target_pairs={{0,2},{1,3},{2,0},{3,1},{4,6},{5,7},{6,4},{7,5},{8,10},{9,11},{10,... | collective-permute-start | bytes 1966088 | tf_op jit(solution)/shard_map/ppermute | solution.py:356
  51.1 3.0 %collective-permute-start.4 = (f32[512,256]{1,0:T(8,128)S(1)}, f32[512,256]{1,0:T(8,128)S(1)}, u32[]{:S(2)}, u32[]{:S(2)}) collective-permute-start(f32[512,256]{1,0:T(8,128)S(1)} %pad_maximum_fusion), channel_id=1, source_target_pairs={{0,16},{4,20},{8,24},{12,28},{16,0},{20,4},{24,8},{28,12},{1,17},{... | collective-permute-start | bytes 1572872 | tf_op jit(solution)/shard_map/ppermute | solution.py:356
  54.0 8.4 %pair_step.2 = (f32[256,256]{1,0:T(8,128)}, f32[256,512]{1,0:T(8,128)}, f32[512,512]{1,0:T(8,128)}) custom-call(s32[1]{0:T(128)} %bitcast.bit_ref, f32[128,1280]{1,0:T(8,128)} %bitcast_dynamic-update-slice_fusion.own_ref, f32[128,1280]{1,0:T(8,128)} %collective-permute-done.other_ref), custom_call_target="tpu_custom_call" | custom-call | flops 3355443200 | bytes 4194304 | tf_op jit(solution)/shard_map/pair_step/pallas_call | solution.py:130
  62.4 3.0 %collective-permute-done.5.other_ref = f32[128,1280]{1,0:T(8,128)} collective-permute-done((f32[128,1280]{1,0:T(8,128)}, f32[128,1280]{1,0:T(8,128)}, u32[]{:S(2)}, u32[]{:S(2)}) %collective-permute-start.5) | collective-permute-done | bytes 655392 | tf_op jit(solution)/shard_map/ppermute | solution.py:356
  65.4 8.4 %pair_step.3 = (f32[256,256]{1,0:T(8,128)}, f32[256,512]{1,0:T(8,128)}, f32[512,512]{1,0:T(8,128)}) custom-call(s32[1]{0:T(128)} %bitcast.bit_ref, f32[128,1280]{1,0:T(8,128)} %copy-done.4, f32[128,1280]{1,0:T(8,128)} %collective-permute-done.5.other_ref), custom_call_target="tpu_custom_call" | custom-call | flops 3355443200 | bytes 4194304 | tf_op jit(solution)/shard_map/pair_step/pallas_call | solution.py:130
  73.9 7.4 %collective-permute-done.4.sides_b0_ref = f32[512,256]{1,0:T(8,128)S(1)} collective-permute-done((f32[512,256]{1,0:T(8,128)S(1)}, f32[512,256]{1,0:T(8,128)S(1)}, u32[]{:S(2)}, u32[]{:S(2)}) %collective-permute-start.4) | collective-permute-done | bytes 524320 | tf_op jit(solution)/shard_map/ppermute | solution.py:356
  83.8 1.5 %collective-permute-start.8 = (f32[512,256]{1,0:T(8,128)S(1)}, f32[512,256]{1,0:T(8,128)S(1)}, u32[]{:S(2)}, u32[]{:S(2)}) collective-permute-start(f32[512,256]{1,0:T(8,128)S(1)} %collective-permute-done.4.sides_b0_ref), channel_id=1, source_target_pairs={{0,2},{1,3},{2,0},{3,1},{4,6},{5,7},{6,4},{7,5},{8,10},{9,11},{10,... | collective-permute-start | bytes 1572872 | tf_op jit(solution)/shard_map/ppermute | solution.py:356
  85.3 20.2 %collective-permute-done.7.sides_b1_ref = f32[512,256]{1,0:T(8,128)S(1)} collective-permute-done((f32[512,256]{1,0:T(8,128)S(1)}, f32[512,256]{1,0:T(8,128)S(1)}, u32[]{:S(2)}, u32[]{:S(2)}) %collective-permute-start.7) | collective-permute-done | bytes 524320 | tf_op jit(solution)/shard_map/ppermute | solution.py:356
  105.9 17.4 %block_step.1 = (f32[512,512]{1,0:T(8,128)}, f32[512,512]{1,0:T(8,128)}, f32[512,256]{1,0:T(8,128)}, f32[512,256]{1,0:T(8,128)}, f32[512,256]{1,0:T(8,128)}) custom-call(s32[1]{0:T(128)} %bitcast.bit_ref, f32[512,512]{1,0:T(8,128)} %get-tuple-element.32.own_ref, f32[512,512]{1,0:T(8,128)} %get-tuple-element.33.other_ref, ...), custom_call_target="tpu_custom_call" | custom-call | flops 10066329600 | bytes 7864320 | tf_op jit(solution)/shard_map/block_step/pallas_call | solution.py:199
  124.4 11.9 %merge_step.1 = (f32[512,2048]{1,0:T(8,128)}, f32[32,512]{1,0:T(8,128)}, f32[32,1024]{1,0:T(8,128)}) custom-call(s32[6]{0:T(128)} %stack.27.bits_ref, f32[256,256]{1,0:T(8,128)} %get-tuple-element.27.pair_inv_ref.inv_ref, f32[512,512]{1,0:T(8,128)} %get-tuple-element.36.binv_ref, f32[512,512]{1,0:T(8,128)} %get-tuple-element.37.head_ref, ...), custom_call_target="tpu_custom_call" | custom-call | flops 5033164800 | bytes 15728640 | tf_op jit(solution)/shard_map/merge_step/pallas_call | solution.py:336
  (44 shorter events, 4.3 us)
Async XLA Ops:
  0.6 20.3 %copy-start.2 = (f32[1,1,1024,32]{2,3,1,0:T(8,128)S(1)}, f32[1,1,1024,32]{2,3,1,0:T(8,128)}, u32[]{:S(2)}) copy-start(f32[1,1,1024,32]{2,3,1,0:T(8,128)} %param.4) | copy-start | bytes 393220
  0.6 20.3 %copy-start.3 = (f32[1,1,512,32]{2,3,1,0:T(8,128)S(1)}, f32[1,1,512,32]{2,3,1,0:T(8,128)}, u32[]{:S(2)}) copy-start(f32[1,1,512,32]{2,3,1,0:T(8,128)} %param.5) | copy-start | bytes 196612
  2.6 59.8 %copy-start = (f32[512,512]{1,0:T(8,128)}, f32[512,512]{1,0:T(8,128)S(1)}, u32[]{:S(2)}) copy-start(f32[512,512]{1,0:T(8,128)S(1)} %maximum_maximum_fusion.sides_ref.sides_a_ref) | copy-start | bytes 3145732
  2.7 46.9 %collective-permute-start.2 = (f32[512,512]{1,0:T(8,128)S(1)}, f32[512,512]{1,0:T(8,128)}, u32[]{:S(2)}, u32[]{:S(2)}) collective-permute-start(f32[512,512]{1,0:T(8,128)S(1)} %maximum_maximum_fusion.sides_ref.sides_a_ref), channel_id=1, source_target_pairs={{0,2},{1,3},{2,0},{3,1},{4,6},{5,7},{6,4},{7,5},{8,10},{9,11},{10,... | collective-permute-start | bytes 3145736 | tf_op jit(solution)/shard_map/ppermute | solution.py:356
  17.8 27.9 %collective-permute-start.1 = (f32[128,1280]{1,0:T(8,128)}, f32[128,1280]{1,0:T(8,128)S(1)}, u32[]{:S(2)}, u32[]{:S(2)}) collective-permute-start(f32[128,1280]{1,0:T(8,128)} %bitcast_dynamic-update-slice_fusion.own_ref), channel_id=1, source_target_pairs={{0,2},{1,3},{2,0},{3,1},{4,6},{5,7},{6,4},{7,5},{8,10},{9,11},{10,... | collective-permute-start | bytes 1966088 | tf_op jit(solution)/shard_map/ppermute | solution.py:356
  17.9 31.6 %collective-permute-start = (f32[128,1280]{1,0:T(8,128)}, f32[128,1280]{1,0:T(8,128)}, u32[]{:S(2)}, u32[]{:S(2)}) collective-permute-start(f32[128,1280]{1,0:T(8,128)} %bitcast_dynamic-update-slice_fusion.own_ref), channel_id=1, source_target_pairs={{0,16},{4,20},{8,24},{12,28},{16,0},{20,4},{24,8},{28,12},{1,17},{... | collective-permute-start | bytes 1966088 | tf_op jit(solution)/shard_map/ppermute | solution.py:356
  21.0 41.5 %copy-start.1 = (f32[1536,32]{0,1:T(8,128)}, f32[1536,32]{0,1:T(8,128)S(1)}, u32[]{:S(2)}) copy-start(f32[1536,32]{0,1:T(8,128)S(1)} %bitcast_dynamic-update-slice_fusion.9) | copy-start | bytes 589828
  21.0 24.7 %collective-permute-start.3 = (f32[32,1024]{1,0:T(8,128)S(1)}, f32[32,1024]{1,0:T(8,128)S(1)}, u32[]{:S(2)}, u32[]{:S(2)}) collective-permute-start(f32[32,1024]{1,0:T(8,128)S(1)} %slice.4), channel_id=1, source_target_pairs={{0,2},{1,3},{2,0},{3,1},{4,6},{5,7},{6,4},{7,5},{8,10},{9,11},{10,... | collective-permute-start | bytes 393224 | tf_op jit(solution)/shard_map/ppermute | solution.py:356
  45.7 8.3 %copy-start.9 = (f32[32,1024]{1,0:T(8,128)}, f32[32,1024]{1,0:T(8,128)S(1)}, u32[]{:S(2)}) copy-start(f32[32,1024]{1,0:T(8,128)S(1)} %collective-permute-done.3.data_c_ref) | copy-start | bytes 393220
  45.7 8.3 %copy-start.4 = (f32[128,1280]{1,0:T(8,128)}, f32[128,1280]{1,0:T(8,128)S(1)}, u32[]{:S(2)}) copy-start(f32[128,1280]{1,0:T(8,128)S(1)} %collective-permute-done.1.own_ref) | copy-start | bytes 1966084
  49.5 15.9 %collective-permute-start.5 = (f32[128,1280]{1,0:T(8,128)}, f32[128,1280]{1,0:T(8,128)}, u32[]{:S(2)}, u32[]{:S(2)}) collective-permute-start(f32[128,1280]{1,0:T(8,128)} %collective-permute-done.other_ref), channel_id=1, source_target_pairs={{0,2},{1,3},{2,0},{3,1},{4,6},{5,7},{6,4},{7,5},{8,10},{9,11},{10,... | collective-permute-start | bytes 1966088 | tf_op jit(solution)/shard_map/ppermute | solution.py:356
  51.0 22.9 %collective-permute-start.6 = (f32[32,1024]{1,0:T(8,128)S(1)}, f32[32,1024]{1,0:T(8,128)}, u32[]{:S(2)}, u32[]{:S(2)}) collective-permute-start(f32[32,1024]{1,0:T(8,128)S(1)} %slice.4), channel_id=1, source_target_pairs={{0,16},{4,20},{8,24},{12,28},{16,0},{20,4},{24,8},{28,12},{1,17},{... | collective-permute-start | bytes 393224 | tf_op jit(solution)/shard_map/ppermute | solution.py:356
  51.1 30.3 %collective-permute-start.4 = (f32[512,256]{1,0:T(8,128)S(1)}, f32[512,256]{1,0:T(8,128)S(1)}, u32[]{:S(2)}, u32[]{:S(2)}) collective-permute-start(f32[512,256]{1,0:T(8,128)S(1)} %pad_maximum_fusion), channel_id=1, source_target_pairs={{0,16},{4,20},{8,24},{12,28},{16,0},{20,4},{24,8},{28,12},{1,17},{... | collective-permute-start | bytes 1572872 | tf_op jit(solution)/shard_map/ppermute | solution.py:356
  81.3 42.0 %copy-start.5 = (f32[512,256]{1,0:T(8,128)}, f32[512,256]{1,0:T(8,128)S(1)}, u32[]{:S(2)}) copy-start(f32[512,256]{1,0:T(8,128)S(1)} %collective-permute-done.4.sides_b0_ref) | copy-start | bytes 1572868
  81.3 24.1 %collective-permute-start.7 = (f32[512,256]{1,0:T(8,128)S(1)}, f32[512,256]{1,0:T(8,128)S(1)}, u32[]{:S(2)}, u32[]{:S(2)}) collective-permute-start(f32[512,256]{1,0:T(8,128)S(1)} %pad_maximum_fusion.1), channel_id=1, source_target_pairs={{0,16},{4,20},{8,24},{12,28},{16,0},{20,4},{24,8},{28,12},{1,17},{... | collective-permute-start | bytes 1572872 | tf_op jit(solution)/shard_map/ppermute | solution.py:356
  83.3 40.1 %collective-permute-start.10 = (f32[32,1024]{1,0:T(8,128)}, f32[32,1024]{1,0:T(8,128)S(1)}, u32[]{:S(2)}, u32[]{:S(2)}) collective-permute-start(f32[32,1024]{1,0:T(8,128)} %collective-permute-done.6.data_b_ref), channel_id=1, source_target_pairs={{0,2},{1,3},{2,0},{3,1},{4,6},{5,7},{6,4},{7,5},{8,10},{9,11},{10,... | collective-permute-start | bytes 393224 | tf_op jit(solution)/shard_map/ppermute | solution.py:356
  83.8 39.6 %collective-permute-start.8 = (f32[512,256]{1,0:T(8,128)S(1)}, f32[512,256]{1,0:T(8,128)S(1)}, u32[]{:S(2)}, u32[]{:S(2)}) collective-permute-start(f32[512,256]{1,0:T(8,128)S(1)} %collective-permute-done.4.sides_b0_ref), channel_id=1, source_target_pairs={{0,2},{1,3},{2,0},{3,1},{4,6},{5,7},{6,4},{7,5},{8,10},{9,11},{10,... | collective-permute-start | bytes 1572872 | tf_op jit(solution)/shard_map/ppermute | solution.py:356
  105.5 17.9 %copy-start.6 = (f32[512,256]{1,0:T(8,128)}, f32[512,256]{1,0:T(8,128)S(1)}, u32[]{:S(2)}) copy-start(f32[512,256]{1,0:T(8,128)S(1)} %collective-permute-done.7.sides_b1_ref) | copy-start | bytes 1572868
  105.5 17.9 %collective-permute-start.9 = (f32[512,256]{1,0:T(8,128)S(1)}, f32[512,256]{1,0:T(8,128)S(1)}, u32[]{:S(2)}, u32[]{:S(2)}) collective-permute-start(f32[512,256]{1,0:T(8,128)S(1)} %collective-permute-done.7.sides_b1_ref), channel_id=1, source_target_pairs={{0,2},{1,3},{2,0},{3,1},{4,6},{5,7},{6,4},{7,5},{8,10},{9,11},{10,... | collective-permute-start | bytes 1572872 | tf_op jit(solution)/shard_map/ppermute | solution.py:356
  123.4 0.7 copy-start.10
  123.4 0.8 copy-start.7
  123.4 1.0 copy-start.8

commit v3 on v2

--- a/solution.py
+++ b/solution.py
@@ -103,6 +103,46 @@
         ],
         axis=0,
     )
+
+
+def pack_kernel(sides_ref, map_ref, core_ref, sems):
+    half = core_ref.shape[0]
+    edge = 2 * half
+    first, second = [pl.multiple_of(sides_ref[index] * edge, edge) for index in (0, 1)]
+    pieces = [
+        (first, first, 0, edge),
+        (first + half, first + half, edge, half),
+        (second, second, 3 * half, edge),
+        (second + half, second + half, 3 * half + edge, half),
+        (first, second, 3 * edge, edge),
+        (first + half, second, 4 * edge, edge),
+    ]
+    copies = []
+    for index, (row, col, place, width) in enumerate(pieces):
+        row, col = pl.multiple_of(row, half), pl.multiple_of(col, half)
+        copy = pltpu.make_async_copy(
+            map_ref.at[pl.ds(row, half), pl.ds(col, width)],
+            core_ref.at[:, pl.ds(place, width)],
+            sems.at[index],
+        )
+        copy.start()
+        copies.append(copy)
+    for copy in copies:
+        copy.wait()
+
+
+def pack_step(sides, box_map):
+    edge = box_map.shape[0] // 4
+    return pl.pallas_call(
+        pack_kernel,
+        out_shape=jax.ShapeDtypeStruct((edge // 2, 5 * edge), jnp.float32),
+        in_specs=[SMEM, pl.BlockSpec(memory_space=pl.ANY)],
+        out_specs=VMEM,
+        scratch_shapes=[pltpu.SemaphoreType.DMA((6,))],
+        compiler_params=PARAMS,
+        cost_estimate=pl.CostEstimate(flops=0, bytes_accessed=20 * edge * edge, transcendentals=0),
+        name="pack_step",
+    )(sides, box_map)
 
 
 def pair_kernel(bit_ref, own_ref, other_ref, inv_ref, solve_ref, part_ref, sum_ref, power_ref, joint_ref):
@@ -372,20 +412,8 @@
     def side(values, row):
         return lax.dynamic_slice_in_dim(values, row * edge, edge, 0)
 
-    half = edge // 2
-
-    def halves(row, col, across, down):
-        start = (row * edge + across * half, col * edge + down * half)
-        return lax.dynamic_slice(box_map, start, (half, half))
-
-    def packed(row):
-        return [halves(row, row, 0, 0), halves(row, row, 0, 1), halves(row, row, 1, 1)]
-
-    def strip(number):
-        start = (side_e * edge + number * half, side_i * edge)
-        return lax.dynamic_slice(box_map, start, (half, edge))
-
-    core = jnp.concatenate(packed(side_e) + packed(side_i) + [strip(0), strip(1)], axis=1)
+    core = pack_step(jnp.stack([side_e, side_i]), box_map)
+    core, box_map = lax.optimization_barrier((core, box_map))
     sides_0 = jnp.concatenate([block(side_e, side_0), block(side_i, side_0)], axis=0)
     sides_1 = jnp.concatenate([block(side_e, side_1), block(side_i, side_1)], axis=0)
     sides = jnp.concatenate([sides_0, sides_1], axis=1)
@@ -427,11 +455,11 @@
     sides_b1 = partner(sides_1, "gx")
     shared_d = partner(shared_b, "gy")
     sides_d0 = partner(sides_b0, "gy")
-    sides_d1 = partner(sides_b1, "gy")
-
     binv, head, left, lead_near, lead_far = block_step(
         near, part, part_far, inv, solve, solve_far, sides
     )
+    sides_b1, binv = lax.optimization_barrier((sides_b1, binv))
+    sides_d1 = partner(sides_b1, "gy")
     bits = jnp.stack([bit_x, bit_y, side_e, side_i, side_0, side_1])
     merged_map, merged_flux, box_values = merge_step(
         bits,

time: 137 us -> 134 us (0.978)
  local copies, waits for them, and re-layouts: 15.7 us -> 3.46 us
  waiting for transfers between devices: 57.5 us -> 63.1 us
  Pallas kernels: 46.1 us -> 49.4 us
    unnamed x33 -> x30, local copies, waits for them, and re-layouts: 11.5 us -> 1.04 us
    ppermute x11, waiting for transfers between devices: 57.5 us -> 63.1 us  [partner(): lax.ppermute(value, axis, [(source, source ^ count // 2) for source in ra...]
    pallas_call x0 -> x1, Pallas kernels: none -> 2.73 us  [pack_step(): pl.pallas_call(pack_kernel, out_shape=jax.ShapeDtypeStruct((edge // 2, 5...]
    concatenate x1 -> x0, local copies, waits for them, and re-layouts: 1.6 us -> none  [on_device(): jnp.concatenate(packed(side_e) + packed(side_i) + [strip(0), strip(1)], a...]
  transfers between devices with their start and end apart: 11 -> 11, of which waited for: 5 -> 5; matrix products, arithmetic and copies ran while one was open for 10% -> 1% of each run, Pallas kernels for 25% -> 26%
where the time goes in v3:
time: 134 us
  waiting for transfers between devices  63.1 us (47%)
  Pallas kernels  49.4 us (37%)
  starting transfers between devices  15.1 us (11%)
  local copies, waits for them, and re-layouts  3.46 us (3%)
  other arithmetic  1.94 us (1%)
    ppermute x11, waiting for transfers between devices, partner(): lax.ppermute(value, axis, [(source, source ^ count // 2) for source in ra...  63.1 us
    pallas_call x1, Pallas kernels, block_step(): pl.pallas_call(block_kernel, out_shape=(shape(size, size), shape(size, si...  17.5 us
    pallas_call x2, Pallas kernels, pair_step(): pl.pallas_call(pair_kernel, out_shape=(shape(edge, edge), shape(edge, 2 *...  17.3 us
    ppermute x11, starting transfers between devices, partner(): lax.ppermute(value, axis, [(source, source ^ count // 2) for source in ra...  15.1 us
    pallas_call x1, Pallas kernels, merge_step(): pl.pallas_call(merge_kernel, out_shape=(shape(2 * edge, 8 * edge), shape(...  11.9 us
    pallas_call x1, Pallas kernels, pack_step(): pl.pallas_call(pack_kernel, out_shape=jax.ShapeDtypeStruct((edge // 2, 5...  2.73 us
  transfers between devices with their start and end apart: 11, of which 5 were waited for; matrix products, arithmetic and copies ran while one was open for 1% of the time, Pallas kernels for 26%

profile of v3, /device:TPU:0, one launch (start us, length us, event | category | flops | bytes accessed | tf_op | source)
XLA Modules:
  0.0 134.0 jit_solution(7650374293256093087)
XLA Ops:
  0.7 0.6 pad_add_fusion.sides_ref
  1.3 2.7 %pack_step.1.own_ref = f32[128,1280]{1,0:T(8,128)} custom-call(s32[2]{0:T(128)} %pad_add_fusion.sides_ref, f32[1024,1024]{1,0:T(8,128)} %bitcast.25), custom_call_target="tpu_custom_call" | custom-call | bytes 1310720 | tf_op jit(solution)/shard_map/pack_step/pallas_call | solution.py:136
  4.1 1.7 %fusion = (f32[256,256]{1,0:T(8,128)S(1)}, f32[256,256]{1,0:T(8,128)S(1)}, f32[256,256]{1,0:T(8,128)S(1)}, f32[256,256]{1,0:T(8,128)S(1)}, f32[256,256]{1,0:T(8,...) fusion(f32[1024,1024]{1,0:T(8,128)} %bitcast.26, s32[]{:T(128)S(6)} %select_n.19, ...), kind=kLoop, calls=%fused_computation.10 | loop fusion | bytes 4194320 | tf_op jit(solution)/shard_map/dynamic_slice | solution.py:410
  5.9 3.1 %collective-permute-start.2 = (f32[512,512]{1,0:T(8,128)S(1)}, f32[512,512]{1,0:T(8,128)S(1)}, u32[]{:S(2)}, u32[]{:S(2)}) collective-permute-start(f32[512,512]{1,0:T(8,128)S(1)} %maximum_maximum_fusion.sides_ref.sides_a_ref), channel_id=1, source_target_pairs={{0,2},{1,3},{2,0},{3,1},{4,6},{5,7},{6,4},{7,5},{8,10},{9,11},{10,... | collective-permute-start | bytes 3145736 | tf_op jit(solution)/shard_map/ppermute | solution.py:396
  9.1 3.0 %collective-permute-start = (f32[128,1280]{1,0:T(8,128)S(1)}, f32[128,1280]{1,0:T(8,128)}, u32[]{:S(2)}, u32[]{:S(2)}) collective-permute-start(f32[128,1280]{1,0:T(8,128)S(1)} %copy-done.1), channel_id=1, source_target_pairs={{0,16},{4,20},{8,24},{12,28},{16,0},{20,4},{24,8},{28,12},{1,17},{... | collective-permute-start | bytes 1966088 | tf_op jit(solution)/shard_map/ppermute | solution.py:396
  12.2 1.6 %collective-permute-start.3 = (f32[32,1024]{1,0:T(8,128)S(1)}, f32[32,1024]{1,0:T(8,128)S(1)}, u32[]{:S(2)}, u32[]{:S(2)}) collective-permute-start(f32[32,1024]{1,0:T(8,128)S(1)} %slice.4), channel_id=1, source_target_pairs={{0,2},{1,3},{2,0},{3,1},{4,6},{5,7},{6,4},{7,5},{8,10},{9,11},{10,... | collective-permute-start | bytes 393224 | tf_op jit(solution)/shard_map/ppermute | solution.py:396
  13.8 35.2 %collective-permute-done.3.data_c_ref = f32[32,1024]{1,0:T(8,128)S(1)} collective-permute-done((f32[32,1024]{1,0:T(8,128)S(1)}, f32[32,1024]{1,0:T(8,128)S(1)}, u32[]{:S(2)}, u32[]{:S(2)}) %collective-permute-start.3) | collective-permute-done | bytes 131104 | tf_op jit(solution)/shard_map/ppermute | solution.py:396
  49.0 1.8 %collective-permute-start.5 = (f32[128,1280]{1,0:T(8,128)}, f32[128,1280]{1,0:T(8,128)}, u32[]{:S(2)}, u32[]{:S(2)}) collective-permute-start(f32[128,1280]{1,0:T(8,128)} %collective-permute-done.other_ref), channel_id=1, source_target_pairs={{0,2},{1,3},{2,0},{3,1},{4,6},{5,7},{6,4},{7,5},{8,10},{9,11},{10,... | collective-permute-start | bytes 1966088 | tf_op jit(solution)/shard_map/ppermute | solution.py:396
  50.8 2.6 %collective-permute-start.6 = (f32[32,1024]{1,0:T(8,128)S(1)}, f32[32,1024]{1,0:T(8,128)S(1)}, u32[]{:S(2)}, u32[]{:S(2)}) collective-permute-start(f32[32,1024]{1,0:T(8,128)S(1)} %slice.4), channel_id=1, source_target_pairs={{0,16},{4,20},{8,24},{12,28},{16,0},{20,4},{24,8},{28,12},{1,17},{... | collective-permute-start | bytes 393224 | tf_op jit(solution)/shard_map/ppermute | solution.py:396
  53.5 0.4 collective-permute-start.4
  53.9 8.9 %pair_step.2 = (f32[256,256]{1,0:T(8,128)}, f32[256,512]{1,0:T(8,128)}, f32[512,512]{1,0:T(8,128)}) custom-call(s32[1]{0:T(128)} %bitcast.bit_ref, f32[128,1280]{1,0:T(8,128)} %pack_step.1.own_ref, f32[128,1280]{1,0:T(8,128)} %collective-permute-done.other_ref), custom_call_target="tpu_custom_call" | custom-call | flops 3355443200 | bytes 4194304 | tf_op jit(solution)/shard_map/pair_step/pallas_call | solution.py:170
  62.8 2.5 %collective-permute-done.5.other_ref = f32[128,1280]{1,0:T(8,128)} collective-permute-done((f32[128,1280]{1,0:T(8,128)}, f32[128,1280]{1,0:T(8,128)}, u32[]{:S(2)}, u32[]{:S(2)}) %collective-permute-start.5) | collective-permute-done | bytes 655392 | tf_op jit(solution)/shard_map/ppermute | solution.py:396
  65.3 8.4 %pair_step.3 = (f32[256,256]{1,0:T(8,128)}, f32[256,512]{1,0:T(8,128)}, f32[512,512]{1,0:T(8,128)}) custom-call(s32[1]{0:T(128)} %bitcast.bit_ref, f32[128,1280]{1,0:T(8,128)} %copy-done.6, f32[128,1280]{1,0:T(8,128)} %collective-permute-done.5.other_ref), custom_call_target="tpu_custom_call" | custom-call | flops 3355443200 | bytes 4194304 | tf_op jit(solution)/shard_map/pair_step/pallas_call | solution.py:170
  73.8 7.5 %collective-permute-done.4.sides_b0_ref = f32[512,256]{1,0:T(8,128)} collective-permute-done((f32[512,256]{1,0:T(8,128)S(1)}, f32[512,256]{1,0:T(8,128)}, u32[]{:S(2)}, u32[]{:S(2)}) %collective-permute-start.4) | collective-permute-done | bytes 524320 | tf_op jit(solution)/shard_map/ppermute | solution.py:396
  81.2 0.6 collective-permute-start.8
  81.8 17.5 %block_step.1 = (f32[512,512]{1,0:T(8,128)}, f32[512,512]{1,0:T(8,128)}, f32[512,256]{1,0:T(8,128)}, f32[512,256]{1,0:T(8,128)}, f32[512,256]{1,0:T(8,128)}) custom-call(s32[1]{0:T(128)} %bitcast.bit_ref, f32[512,512]{1,0:T(8,128)} %get-tuple-element.39.own_ref, f32[512,512]{1,0:T(8,128)} %get-tuple-element.40.other_ref, ...), custom_call_target="tpu_custom_call" | custom-call | flops 10066329600 | bytes 7864320 | tf_op jit(solution)/shard_map/block_step/pallas_call | solution.py:239
  99.3 6.9 %collective-permute-done.7.sides_b1_ref = f32[512,256]{1,0:T(8,128)S(1)} collective-permute-done((f32[512,256]{1,0:T(8,128)S(1)}, f32[512,256]{1,0:T(8,128)S(1)}, u32[]{:S(2)}, u32[]{:S(2)}) %collective-permute-start.7) | collective-permute-done | bytes 524320 | tf_op jit(solution)/shard_map/ppermute | solution.py:396
  106.2 0.6 collective-permute-start.9
  106.8 0.7 stack.32.bits_ref
  107.5 1.4 %collective-permute-start.10 = (f32[32,1024]{1,0:T(8,128)S(1)}, f32[32,1024]{1,0:T(8,128)S(1)}, u32[]{:S(2)}, u32[]{:S(2)}) collective-permute-start(f32[32,1024]{1,0:T(8,128)S(1)} %collective-permute-done.6.data_b_ref), channel_id=1, source_target_pairs={{0,2},{1,3},{2,0},{3,1},{4,6},{5,7},{6,4},{7,5},{8,10},{9,11},{10,... | collective-permute-start | bytes 393224 | tf_op jit(solution)/shard_map/ppermute | solution.py:396
  108.9 1.2 maximum_maximum_fusion.1.kept_ref
  110.1 10.9 %collective-permute-done.10.data_d_ref = f32[32,1024]{1,0:T(8,128)S(1)} collective-permute-done((f32[32,1024]{1,0:T(8,128)S(1)}, f32[32,1024]{1,0:T(8,128)S(1)}, u32[]{:S(2)}, u32[]{:S(2)}) %collective-permute-start.10) | collective-permute-done | bytes 131104 | tf_op jit(solution)/shard_map/ppermute | solution.py:396
  121.0 0.6 copy-done.12
  122.0 11.9 %merge_step.1 = (f32[512,2048]{1,0:T(8,128)}, f32[32,512]{1,0:T(8,128)}, f32[32,1024]{1,0:T(8,128)}) custom-call(s32[6]{0:T(128)} %stack.32.bits_ref, f32[256,256]{1,0:T(8,128)} %get-tuple-element.33.pair_inv_ref.inv_ref, f32[512,512]{1,0:T(8,128)} %get-tuple-element.44.binv_ref, f32[512,512]{1,0:T(8,128)} %get-tuple-element.45.head_ref, ...), custom_call_target="tpu_custom_call" | custom-call | flops 5033164800 | bytes 15728640 | tf_op jit(solution)/shard_map/merge_step/pallas_call | solution.py:376
  (42 shorter events, 0.7 us)
Async XLA Ops:
  4.0 5.0 %copy-start.1 = (f32[128,1280]{1,0:T(8,128)S(1)}, f32[128,1280]{1,0:T(8,128)}, u32[]{:S(2)}) copy-start(f32[128,1280]{1,0:T(8,128)} %pack_step.1.own_ref) | copy-start | bytes 1966084
  4.0 8.1 %copy-start.3 = (f32[1,1,1024,32]{2,3,1,0:T(8,128)S(1)}, f32[1,1,1024,32]{2,3,1,0:T(8,128)}, u32[]{:S(2)}) copy-start(f32[1,1,1024,32]{2,3,1,0:T(8,128)} %param.4) | copy-start | bytes 393220
  4.0 8.1 %copy-start.4 = (f32[1,1,512,32]{2,3,1,0:T(8,128)S(1)}, f32[1,1,512,32]{2,3,1,0:T(8,128)}, u32[]{:S(2)}) copy-start(f32[1,1,512,32]{2,3,1,0:T(8,128)} %param.5) | copy-start | bytes 196612
  5.9 56.9 %copy-start = (f32[512,512]{1,0:T(8,128)}, f32[512,512]{1,0:T(8,128)S(1)}, u32[]{:S(2)}) copy-start(f32[512,512]{1,0:T(8,128)S(1)} %maximum_maximum_fusion.sides_ref.sides_a_ref) | copy-start | bytes 3145732
  5.9 43.1 %collective-permute-start.2 = (f32[512,512]{1,0:T(8,128)S(1)}, f32[512,512]{1,0:T(8,128)S(1)}, u32[]{:S(2)}, u32[]{:S(2)}) collective-permute-start(f32[512,512]{1,0:T(8,128)S(1)} %maximum_maximum_fusion.sides_ref.sides_a_ref), channel_id=1, source_target_pairs={{0,2},{1,3},{2,0},{3,1},{4,6},{5,7},{6,4},{7,5},{8,10},{9,11},{10,... | collective-permute-start | bytes 3145736 | tf_op jit(solution)/shard_map/ppermute | solution.py:396
  9.0 40.0 %collective-permute-start.1 = (f32[128,1280]{1,0:T(8,128)S(1)}, f32[128,1280]{1,0:T(8,128)S(1)}, u32[]{:S(2)}, u32[]{:S(2)}) collective-permute-start(f32[128,1280]{1,0:T(8,128)S(1)} %copy-done.1), channel_id=1, source_target_pairs={{0,2},{1,3},{2,0},{3,1},{4,6},{5,7},{6,4},{7,5},{8,10},{9,11},{10,... | collective-permute-start | bytes 1966088 | tf_op jit(solution)/shard_map/ppermute | solution.py:396
  9.1 39.9 %collective-permute-start = (f32[128,1280]{1,0:T(8,128)S(1)}, f32[128,1280]{1,0:T(8,128)}, u32[]{:S(2)}, u32[]{:S(2)}) collective-permute-start(f32[128,1280]{1,0:T(8,128)S(1)} %copy-done.1), channel_id=1, source_target_pairs={{0,16},{4,20},{8,24},{12,28},{16,0},{20,4},{24,8},{28,12},{1,17},{... | collective-permute-start | bytes 1966088 | tf_op jit(solution)/shard_map/ppermute | solution.py:396
  12.2 50.6 %copy-start.2 = (f32[1536,32]{0,1:T(8,128)}, f32[1536,32]{0,1:T(8,128)S(1)}, u32[]{:S(2)}) copy-start(f32[1536,32]{0,1:T(8,128)S(1)} %bitcast_dynamic-update-slice_fusion.1) | copy-start | bytes 589828
  12.2 36.8 %collective-permute-start.3 = (f32[32,1024]{1,0:T(8,128)S(1)}, f32[32,1024]{1,0:T(8,128)S(1)}, u32[]{:S(2)}, u32[]{:S(2)}) collective-permute-start(f32[32,1024]{1,0:T(8,128)S(1)} %slice.4), channel_id=1, source_target_pairs={{0,2},{1,3},{2,0},{3,1},{4,6},{5,7},{6,4},{7,5},{8,10},{9,11},{10,... | collective-permute-start | bytes 393224 | tf_op jit(solution)/shard_map/ppermute | solution.py:396
  49.0 24.8 %copy-start.10 = (f32[32,1024]{1,0:T(8,128)}, f32[32,1024]{1,0:T(8,128)S(1)}, u32[]{:S(2)}) copy-start(f32[32,1024]{1,0:T(8,128)S(1)} %collective-permute-done.3.data_c_ref) | copy-start | bytes 393220
  49.0 4.9 %copy-start.6 = (f32[128,1280]{1,0:T(8,128)}, f32[128,1280]{1,0:T(8,128)S(1)}, u32[]{:S(2)}) copy-start(f32[128,1280]{1,0:T(8,128)S(1)} %collective-permute-done.1.own_ref) | copy-start | bytes 1966084
  49.0 4.8 %copy-start.5 = (f32[512,512]{1,0:T(8,128)}, f32[512,512]{1,0:T(8,128)S(1)}, u32[]{:S(2)}) copy-start(f32[512,512]{1,0:T(8,128)S(1)} %collective-permute-done.2.sides_c_ref) | copy-start | bytes 3145732
  49.0 16.3 %collective-permute-start.5 = (f32[128,1280]{1,0:T(8,128)}, f32[128,1280]{1,0:T(8,128)}, u32[]{:S(2)}, u32[]{:S(2)}) collective-permute-start(f32[128,1280]{1,0:T(8,128)} %collective-permute-done.other_ref), channel_id=1, source_target_pairs={{0,2},{1,3},{2,0},{3,1},{4,6},{5,7},{6,4},{7,5},{8,10},{9,11},{10,... | collective-permute-start | bytes 1966088 | tf_op jit(solution)/shard_map/ppermute | solution.py:396
  50.8 22.9 %collective-permute-start.6 = (f32[32,1024]{1,0:T(8,128)S(1)}, f32[32,1024]{1,0:T(8,128)S(1)}, u32[]{:S(2)}, u32[]{:S(2)}) collective-permute-start(f32[32,1024]{1,0:T(8,128)S(1)} %slice.4), channel_id=1, source_target_pairs={{0,16},{4,20},{8,24},{12,28},{16,0},{20,4},{24,8},{28,12},{1,17},{... | collective-permute-start | bytes 393224 | tf_op jit(solution)/shard_map/ppermute | solution.py:396
  53.5 27.8 %collective-permute-start.4 = (f32[512,256]{1,0:T(8,128)S(1)}, f32[512,256]{1,0:T(8,128)}, u32[]{:S(2)}, u32[]{:S(2)}) collective-permute-start(f32[512,256]{1,0:T(8,128)S(1)} %pad_maximum_fusion), channel_id=1, source_target_pairs={{0,16},{4,20},{8,24},{12,28},{16,0},{20,4},{24,8},{28,12},{1,17},{... | collective-permute-start | bytes 1572872 | tf_op jit(solution)/shard_map/ppermute | solution.py:396
  73.8 33.7 %copy-start.11 = (f32[32,1024]{1,0:T(8,128)}, f32[32,1024]{1,0:T(8,128)S(1)}, u32[]{:S(2)}) copy-start(f32[32,1024]{1,0:T(8,128)S(1)} %collective-permute-done.6.data_b_ref) | copy-start | bytes 393220
  81.2 25.0 %collective-permute-start.7 = (f32[512,256]{1,0:T(8,128)S(1)}, f32[512,256]{1,0:T(8,128)S(1)}, u32[]{:S(2)}, u32[]{:S(2)}) collective-permute-start(f32[512,256]{1,0:T(8,128)S(1)} %pad_maximum_fusion.1), channel_id=1, source_target_pairs={{0,16},{4,20},{8,24},{12,28},{16,0},{20,4},{24,8},{28,12},{1,17},{... | collective-permute-start | bytes 1572872 | tf_op jit(solution)/shard_map/ppermute | solution.py:396
  81.2 39.8 %collective-permute-start.8 = (f32[512,256]{1,0:T(8,128)}, f32[512,256]{1,0:T(8,128)S(1)}, u32[]{:S(2)}, u32[]{:S(2)}) collective-permute-start(f32[512,256]{1,0:T(8,128)} %collective-permute-done.4.sides_b0_ref), channel_id=1, source_target_pairs={{0,2},{1,3},{2,0},{3,1},{4,6},{5,7},{6,4},{7,5},{8,10},{9,11},{10,... | collective-permute-start | bytes 1572872 | tf_op jit(solution)/shard_map/ppermute | solution.py:396
  106.2 14.8 %copy-start.7 = (f32[512,256]{1,0:T(8,128)}, f32[512,256]{1,0:T(8,128)S(1)}, u32[]{:S(2)}) copy-start(f32[512,256]{1,0:T(8,128)S(1)} %collective-permute-done.7.sides_b1_ref) | copy-start | bytes 1572868
  106.2 14.8 %collective-permute-start.9 = (f32[512,256]{1,0:T(8,128)S(1)}, f32[512,256]{1,0:T(8,128)S(1)}, u32[]{:S(2)}, u32[]{:S(2)}) collective-permute-start(f32[512,256]{1,0:T(8,128)S(1)} %collective-permute-done.7.sides_b1_ref), channel_id=1, source_target_pairs={{0,2},{1,3},{2,0},{3,1},{4,6},{5,7},{6,4},{7,5},{8,10},{9,11},{10,... | collective-permute-start | bytes 1572872 | tf_op jit(solution)/shard_map/ppermute | solution.py:396
  107.5 13.5 %collective-permute-start.10 = (f32[32,1024]{1,0:T(8,128)S(1)}, f32[32,1024]{1,0:T(8,128)S(1)}, u32[]{:S(2)}, u32[]{:S(2)}) collective-permute-start(f32[32,1024]{1,0:T(8,128)S(1)} %collective-permute-done.6.data_b_ref), channel_id=1, source_target_pairs={{0,2},{1,3},{2,0},{3,1},{4,6},{5,7},{6,4},{7,5},{8,10},{9,11},{10,... | collective-permute-start | bytes 393224 | tf_op jit(solution)/shard_map/ppermute | solution.py:396
  121.0 0.7 copy-start.12
  121.0 0.8 copy-start.8
  121.0 1.0 copy-start.9
